TPU v7x, 256 devices: a whole 4x4x8 slice. The times are simulated.
256 devices in a mesh: dp: 8 (over z), seq: 32 (over y, x, core).
Axes of the slice: x: 4, y: 4, z: 8, core: 2. Of those that a mesh axis runs over, the one named last changes fastest.
Arguments:
- embeddings: bfloat16 [8, 16384, 512], P('dp', 'seq'), may hold values from -6 to 6
- user_ids: int32 [8, 16384], P('dp', 'seq'), may hold values from 0 to 63, never falling along the last dimension, each value on 1 to 512 neighbouring positions
- time_gaps: int32 [8, 16384], P('dp', 'seq'), may hold values from 0 to 16
- proj_weight: bfloat16 [512, 2048], replicated, may hold values from -0.25 to 0.25
- out_weight: bfloat16 [512, 512], replicated, may hold values from -0.25 to 0.25
- frequencies: float32 [64], replicated, may hold values from 0.001 to 0.1
- time_mix: float32 [4, 64], replicated, may hold values from -0.9 to 0.9
- cotangent: bfloat16 [8, 16384, 512], P('dp', 'seq'), may hold values from -6 to 6
Outputs:
- layer_out: bfloat16 [8, 16384, 512], P('dp', 'seq')
- grad_input: bfloat16 [8, 16384, 512], P('dp', 'seq')
- grad_proj: float32 [512, 2048], P('seq')
- grad_out_weight: float32 [512, 512], P('seq')
- grad_time_mix: float32 [4, 64], replicated
Inputs may be any that keep to these rules, and one draw needn't show every extreme that they name: `user_ids`: within a stream the ids never fall, so each user's events are consecutive; a user holds at most 512 events, and some user holds exactly that many.
All inputs are finite; a program needn't handle non-finite values.
Results may differ from a plain program's by a relative error of at most 0.019.
Values may be sent and summed in bfloat16 or wider, within the bound.
A program may use at most 64 MiB of HBM per device.

v0:
```python
import jax
import jax.numpy as jnp
from jax import lax
from jax.sharding import PartitionSpec as P

BLOCK = 512
REACH = 1


EPSILON = 1e-05
HIGH = lax.Precision.HIGHEST


def entering(value, axis, join, neutral):
    count, mine = (lax.axis_size(axis), lax.axis_index(axis))
    pieces = jax.tree.map(lambda part: lax.all_gather(part, axis), value)
    total = jax.tree.map(
        lambda part, zero: jnp.full_like(part, 0) + jnp.asarray(zero, part.dtype), value, neutral
    )

    def turn(position, total):
        longer = join(total, jax.tree.map(lambda part: part[position], pieces))
        return jax.tree.map(lambda new, old: jnp.where(position < mine, new, old), longer, total)

    return lax.fori_loop(0, count - 1, turn, total)


def shifted(array, axis, by):
    length = lax.axis_size(axis)
    pairs = [(i, i + by) for i in range(length) if 0 <= i + by < length]
    return lax.ppermute(array, axis, pairs)


def silu_slope(value):
    sigma = jax.nn.sigmoid(value)
    return sigma * (1.0 + value * (1.0 - sigma))


def run_times(users, gaps):
    count = users.shape[0]
    running = jnp.cumsum(gaps)
    position = jnp.arange(count, dtype=jnp.int32)
    before = jnp.concatenate([users[:1] - 1, users[:-1]])
    opening = jnp.where(users != before, position, 0)
    first = lax.cummax(opening, axis=0)
    return running - (running[first] - gaps[first])


def combine(earlier, later):
    valid_a, user_a, total_a, whole_a = earlier
    valid_b, user_b, total_b, whole_b = later
    both = (valid_a == 1) & (valid_b == 1)
    has_later = valid_b == 1
    same = user_a == user_b
    joined = jnp.where((whole_b == 1) & same, total_a + total_b, total_b)
    merged_whole = jnp.where((whole_a == 1) & (whole_b == 1) & same, 1, 0)
    return (
        jnp.maximum(valid_a, valid_b).astype(jnp.int32),
        jnp.where(has_later, user_b, user_a).astype(jnp.int32),
        jnp.where(both, joined, jnp.where(has_later, total_b, total_a)).astype(jnp.int32),
        jnp.where(both, merged_whole, jnp.where(has_later, whole_b, whole_a)).astype(jnp.int32),
    )


def time_features(times, frequencies, time_mix):
    angles = times.astype(jnp.float32)[:, None] * frequencies[None, :]
    cosines = jnp.cos(angles)
    sines = jnp.sin(angles)
    key_time = jnp.concatenate([cosines, sines], 1).astype(jnp.bfloat16)
    query_time = jnp.concatenate(
        [cosines[:, None, :] * time_mix[None], sines[:, None, :] * time_mix[None]], 2
    ).astype(jnp.bfloat16)
    return (cosines, sines, key_time, query_time)


def project(events, proj_weight):
    values_wide = events.astype(jnp.float32)
    scale_in = lax.rsqrt(jnp.mean(values_wide * values_wide, -1, keepdims=True) + EPSILON)
    unit_rows = values_wide * scale_in
    normed = unit_rows.astype(jnp.bfloat16)
    preact = jnp.dot(normed, proj_weight, preferred_element_type=jnp.float32)
    hidden = jax.nn.silu(preact).astype(jnp.bfloat16)
    return (scale_in, unit_rows, normed, preact, hidden)


def pair_scores(query, query_time, keys, key_time):
    inverse = query.shape[-1] ** (-0.5)
    return jnp.einsum(
        "qhd,khd->hqk", query, keys, preferred_element_type=jnp.float32
    ) * inverse + jnp.einsum(
        "qhf,kf->hqk", query_time, key_time, preferred_element_type=jnp.float32
    )


def pair_mask(query_user, query_pos, key_user, key_pos):
    return (
        (key_user[None, :] == query_user[:, None])
        & (key_pos[None, :] <= query_pos[:, None])
        & (key_pos[None, :] >= 0)
    )


def forward_pair(operands):
    query, query_time, query_user, query_pos, keys, values, key_time, key_user, key_pos = operands
    mask = pair_mask(query_user, query_pos, key_user, key_pos)
    scores = pair_scores(query, query_time, keys, key_time)
    weights = jnp.where(mask[None], jax.nn.silu(scores), 0.0).astype(jnp.bfloat16)
    return jnp.einsum("hqk,khd->qhd", weights, values, preferred_element_type=jnp.float32)


def forward_none(operands):
    return jnp.zeros(operands[0].shape, jnp.float32)


def backward_pair(operands):
    (
        query,
        query_time,
        query_user,
        query_pos,
        grad_tile,
        keys,
        values,
        key_time,
        key_user,
        key_pos,
    ) = operands
    inverse = query.shape[-1] ** (-0.5)
    mask = pair_mask(query_user, query_pos, key_user, key_pos)
    scores = pair_scores(query, query_time, keys, key_time)
    weights = jnp.where(mask[None], jax.nn.silu(scores), 0.0).astype(jnp.bfloat16)
    grad_weights = jnp.einsum("qhd,khd->hqk", grad_tile, values, preferred_element_type=jnp.float32)
    grad_scores = jnp.where(mask[None], grad_weights * silu_slope(scores), 0.0).astype(jnp.bfloat16)
    value_part = jnp.einsum("hqk,qhd->khd", weights, grad_tile, preferred_element_type=jnp.float32)
    key_part = (
        jnp.einsum("hqk,qhd->khd", grad_scores, query, preferred_element_type=jnp.float32) * inverse
    )
    query_part = (
        jnp.einsum("hqk,khd->qhd", grad_scores, keys, preferred_element_type=jnp.float32) * inverse
    )
    qtime_part = jnp.einsum(
        "hqk,kf->qhf", grad_scores, key_time, preferred_element_type=jnp.float32
    )
    return (query_part, qtime_part, key_part, value_part)


def backward_none(operands):
    return (
        jnp.zeros(operands[0].shape, jnp.float32),
        jnp.zeros(operands[1].shape, jnp.float32),
        jnp.zeros(operands[5].shape, jnp.float32),
        jnp.zeros(operands[6].shape, jnp.float32),
    )


def body(
    embeddings, user_ids, time_gaps, proj_weight, out_weight, frequencies, time_mix, cotangent
):
    events = embeddings[0]
    users = user_ids[0]
    gaps = time_gaps[0]
    upstream = cotangent[0]
    count = events.shape[0]
    model_width = events.shape[1]
    heads = time_mix.shape[0]
    head_size = model_width // heads
    freq_count = frequencies.shape[0]
    device = lax.axis_index("seq")
    seq_devices = lax.axis_size("seq")
    local_times = run_times(users, gaps)
    summary = (
        jnp.ones((1,), jnp.int32),
        users[-1:],
        local_times[-1:],
        (users[:1] == users[-1:]).astype(jnp.int32),
    )
    identity = (
        jnp.zeros((1,), jnp.int32),
        jnp.zeros((1,), jnp.int32),
        jnp.zeros((1,), jnp.int32),
        jnp.zeros((1,), jnp.int32),
    )
    carried = entering(summary, "seq", combine, identity)
    times = (
        local_times + jnp.where((carried[0] == 1) & (users == carried[1]), carried[2], 0)
    ).astype(jnp.int32)
    cosines, sines, key_time, query_time = time_features(times, frequencies, time_mix)
    scale_in, unit_rows, normed, preact, hidden = project(events, proj_weight)
    gate_part = hidden[:, :model_width]
    value_flat = hidden[:, model_width : 2 * model_width]
    query_flat = hidden[:, 2 * model_width : 3 * model_width]
    key_flat = hidden[:, 3 * model_width :]
    user_marks = users.astype(jnp.bfloat16)
    positions = device * count + jnp.arange(count, dtype=jnp.int32)
    sources = []
    distance = 1
    received = shifted((key_flat, value_flat, key_time, user_marks), "seq", distance)
    sources.append(
        (received[0], received[1], received[2], received[3], positions - distance * count)
    )
    sources.append((key_flat, value_flat, key_time, user_marks, positions))

    def head_tile(flat):
        return flat.reshape(BLOCK, heads, head_size)

    def key_operands(source_index):
        keys, values, times_part, marks, places = sources[source_index]
        return (head_tile(keys), head_tile(values), times_part, marks, places)

    def query_operands():
        return (head_tile(query_flat), query_time, user_marks, positions)

    def candidates():
        listed = []
        tile_index = 0
        listed.append((0, tile_index))
        tile_index = 0
        listed.append((REACH, tile_index))
        return listed

    def is_live(query_part, key_part):
        return (key_part[3][-1] >= query_part[2][0]) & (key_part[4][-1] >= 0)

    query_part = query_operands()
    total = jnp.zeros((BLOCK, heads, head_size), jnp.float32)
    for pair in candidates():
        key_part = key_operands(pair[0])
        total = total + lax.cond(
            is_live(query_part, key_part), forward_pair, forward_none, query_part + key_part
        )
    attended = total.reshape(count, model_width)
    scale_mid = lax.rsqrt(jnp.mean(attended * attended, -1, keepdims=True) + EPSILON)
    normed_mid = attended * scale_mid
    gate_wide = gate_part.astype(jnp.float32)
    gated = (normed_mid * gate_wide).astype(jnp.bfloat16)
    layer_out = (
        events.astype(jnp.float32) + jnp.dot(gated, out_weight, preferred_element_type=jnp.float32)
    ).astype(jnp.bfloat16)
    grad_gated = jnp.einsum("ef,df->ed", upstream, out_weight, preferred_element_type=jnp.float32)
    grad_gate = grad_gated * normed_mid
    grad_mid = grad_gated * gate_wide
    grad_attended = (
        scale_mid * (grad_mid - normed_mid * jnp.mean(grad_mid * normed_mid, -1, keepdims=True))
    ).astype(jnp.bfloat16)
    key_grads = {}
    query_part = query_operands()
    grad_tile = head_tile(grad_attended)
    grad_query = jnp.zeros((BLOCK, heads, head_size), jnp.float32)
    grad_qtime = jnp.zeros((BLOCK, heads, 2 * freq_count), jnp.float32)
    for pair in candidates():
        key_part = key_operands(pair[0])
        result = lax.cond(
            is_live(query_part, key_part),
            backward_pair,
            backward_none,
            query_part + (grad_tile,) + key_part,
        )
        grad_query = grad_query + result[0]
        grad_qtime = grad_qtime + result[1]
        key_grads[pair] = (result[2], result[3])

    def source_grads(source_index):
        keys_part = key_grads[source_index, 0][0]
        values_part = key_grads[source_index, 0][1]
        return (keys_part.reshape(count, model_width), values_part.reshape(count, model_width))

    grad_keys_flat, grad_values_flat = source_grads(REACH)
    distance = 1
    partial_keys, partial_values = source_grads(distance - 1)
    returned = (
        shifted(partial_keys.astype(jnp.bfloat16), "seq", -distance).astype(partial_keys.dtype),
        shifted(partial_values.astype(jnp.bfloat16), "seq", -distance).astype(partial_values.dtype),
    )
    grad_keys_flat = grad_keys_flat + returned[0]
    grad_values_flat = grad_values_flat + returned[1]
    grad_query_flat = grad_query.reshape(count, model_width)
    grad_act = jnp.concatenate([grad_gate, grad_values_flat, grad_query_flat, grad_keys_flat], 1)
    grad_pre = (grad_act * silu_slope(preact)).astype(jnp.bfloat16)
    grad_normed = jnp.einsum("ef,df->ed", grad_pre, proj_weight, preferred_element_type=jnp.float32)
    grad_input = (
        upstream.astype(jnp.float32)
        + scale_in
        * (grad_normed - unit_rows * jnp.mean(grad_normed * unit_rows, -1, keepdims=True))
    ).astype(jnp.bfloat16)
    proj_part = jnp.einsum("ed,ef->df", normed, grad_pre, preferred_element_type=jnp.float32)
    out_part = jnp.einsum("ed,ef->df", gated, upstream, preferred_element_type=jnp.float32)
    whole = lax.psum(jnp.concatenate([proj_part, out_part], 1).astype(jnp.bfloat16), "dp")
    shard = lax.psum_scatter(whole, "seq", scatter_dimension=0, tiled=True).astype(jnp.float32)
    grad_mix = jnp.einsum(
        "ehf,ef->hf", grad_qtime[:, :, :freq_count], cosines, precision=HIGH
    ) + jnp.einsum("ehf,ef->hf", grad_qtime[:, :, freq_count:], sines, precision=HIGH)
    grad_mix = lax.psum(grad_mix, ("dp", "seq"))
    factor = float(lax.axis_size("dp") * seq_devices * count) ** (-0.5)
    grad_proj = shard[:, : 4 * model_width] * factor
    grad_out_weight = shard[:, 4 * model_width :] * factor
    return (layer_out[None], grad_input[None], grad_proj, grad_out_weight, grad_mix * factor)


def solution(mesh):
    return jax.shard_map(
        body,
        mesh=mesh,
        in_specs=(
            P("dp", "seq", None),
            P("dp", "seq"),
            P("dp", "seq"),
            P(),
            P(),
            P(),
            P(),
            P("dp", "seq", None),
        ),
        out_specs=(P("dp", "seq", None), P("dp", "seq", None), P("seq", None), P("seq", None), P()),
        check_vma=False,
    )
```

profile of v0, /device:TPU:6, one launch (start us, length us, event | category | flops | bytes accessed | tf_op | source)
XLA Modules:
  0.0 554.6 jit_solution(1448338192975510792)
XLA Ops:
  16.0 3.6 gather_fusion.1
  19.7 3.5 gather_fusion
  27.3 15.7 %all-reduce.4 = (s32[32]{0:T(128)S(1)}, s32[32]{0:T(128)S(1)}, s32[32]{0:T(128)S(1)}, s32[32]{0:T(128)S(1)}) all-reduce(s32[32]{0:T(128)S(1)} %dynamic-update-slice, s32[32]{0:T(128)S(1)} %bitcast_dynamic-update-slice_fusion.1, s32[32]{0:T(128)S(1)} %bitcast_dynamic-update-slice_fusion, ...), channel_id=1, replica_groups=mesh['dp'=8,'seq'=32] {'seq'}, use_global_device_ids=true, to_apply=%add | all-reduce | flops 128 | bytes 1024
  43.1 217.0 %while.17 = (s32[]{:T(128)}, s32[1]{0:T(128)}, s32[1]{0:T(128)}, s32[1]{0:T(128)}, s32[]{:T(128)}, /*index=5*/s32[32,1]{0,1:T(1,128)S(1)}, s32[32,1]{0,1:T(1,128...) while((s32[]{:T(128)}, s32[1]{0:T(128)}, s32[1]{0:T(128)}, s32[1]{0:T(128)}, ...), condition=%wide.region_6.7_spmd, body=%wide.region_5.6_spmd.sunk | while | flops 18 | bytes 315 | solution.py:25
  264.2 3.6 multiply_convert_fusion
  270.4 4.0 collective-permute-start.3
  287.3 10.0 %conditional.5 = (f32[512,4,128]{2,0,1:T(8,128)}) conditional(s32[]{:T(128)} %bitcast.54, () %tuple.57, (bf16[512]{0:T(512)(128)(2,1)S(1)}, s32[512]{0:T(512)S(1)}, bf16[512,4,128]{2,1,0:T(4,128)(2,1)S(1)}, bf16[512,4,128]{2,1,0:T(4,128)(2,1)}, bf16[512,128]{1,0:T(8,128)(2,1)S(1)}, /*index=5*/bf16[512,4,128]{2,0,1:T(8,128)(2,1)S(1)}, ...), branch_computations={%region_9.10_spmd, %region_10.11_spmd} | conditional | flops 815268352 | bytes 12195848 | solution.py:228
  288.4 3.7 fusion.14
  292.1 5.2 fusion.12
  303.8 10.7 %conditional.4 = (f32[512,4,128]{2,0,1:T(8,128)}) conditional(s32[]{:T(128)} %bitcast.31, () %tuple.54, (bf16[512]{0:T(512)(128)(2,1)}, bf16[512]{0:T(512)(128)(2,1)S(1)}, s32[512]{0:T(512)S(1)}, s32[512]{0:T(512)S(1)}, bf16[512,4,128]{2,1,0:T(4,128)(2,1)S(1)}, /*index=5*/bf16[512,4,128]{2,1,0:T(4,128)(2,1)}, bf16[512,128]{1,0:T(8,128)(2,1)}, ...), branch_computations={%region_7.8_spmd, %region_8.9_spmd} | conditional | flops 815268352 | bytes 12198920 | solution.py:228
  305.5 3.7 fusion.3
  309.2 5.2 fusion.1
  318.2 2.8 multiply_convert_fusion.1
  322.9 11.7 %conditional.7 = (f32[512,4,128]{2,0,1:T(8,128)S(1)}, f32[512,4,128]{2,0,1:T(8,128)S(1)}, f32[512,4,128]{2,0,1:T(8,128)S(1)}, f32[512,4,128]{2,0,1:T(8,128)S(1)}) conditional(s32[]{:T(128)} %bitcast.31, () %tuple.61, (bf16[512]{0:T(512)(128)(2,1)}, bf16[512]{0:T(512)(128)(2,1)S(1)}, s32[512]{0:T(512)S(1)}, s32[512]{0:T(512)S(1)}, ...), branch_computations={%region_15.16_spmd, %region_16.17_spmd} | conditional | flops 1900020224 | bytes 45098100 | solution.py:252
  336.4 3.6 collective-permute-start.5
  342.0 29.8 %conditional.6 = (f32[512,4,128]{2,0,1:T(8,128)}, f32[512,4,128]{2,0,1:T(8,128)}, f32[512,512]{1,0:T(8,128)}, f32[512,512]{1,0:T(8,128)}) conditional(s32[]{:T(128)} %bitcast.54, () %tuple.59, (bf16[512]{0:T(512)(128)(2,1)S(1)}, s32[512]{0:T(512)S(1)}, bf16[512,4,128]{2,1,0:T(4,128)(2,1)}, bf16[512,4,128]{2,1,0:T(4,128)(2,1)}, ...), branch_computations={%region_13.14_spmd, %region_14.15_spmd} | conditional | flops 1900020224 | bytes 65018056 | solution.py:252
  351.1 4.3 select_convert_fusion.3
  355.4 2.5 copy.107
  357.9 3.6 fusion.23
  364.0 2.6 copy.109
  366.6 3.4 fusion.24
  387.5 79.0 %psum.15 = f32[4,64]{1,0:T(4,128)S(1)} all-reduce(f32[4,64]{1,0:T(4,128)S(1)} %add_bitcast_fusion.3), channel_id=1, replica_groups=mesh['dp'=8,'seq'=32] {'dp','seq'}, use_global_device_ids=true, to_apply=%region_20.21 | all-reduce | flops 256 | bytes 2048 | tf_op jit(solution)/shard_map/psum | solution.py:292
  469.4 3.9 fusion.56
  475.6 69.9 %all-reduce.7.cloned.1.call-done = bf16[16,2560]{1,0:T(8,128)(2,1)} async-done(((bf16[16,2560]{1,0:T(8,128)(2,1)}), bf16[16,2560]{1,0:T(8,128)(2,1)}) %all-reduce.7.cloned.1.call-update) | async-done | bytes 81936 | tf_op jit(solution)/shard_map/psum | solution.py:287
  (246 shorter events, 152.4 us)
Async XLA Ops:
  7.2 257.0 %copy-start = (bf16[512,2048]{1,0:T(8,128)(2,1)S(1)}, bf16[512,2048]{1,0:T(8,128)(2,1)}, u32[]{:S(2)}) copy-start(bf16[512,2048]{1,0:T(8,128)(2,1)} %param.21) | copy-start | bytes 6291460
  7.2 16.0 %copy-start.23 = (u32[256]{0:T(256)S(1)}, u32[256]{0:T(256)}, u32[]{:S(2)}) copy-start(u32[256]{0:T(256)} %constant.130) | copy-start | bytes 3076
  7.2 252.9 %copy-start.20 = (s32[1,512]{1,0:T(1,128)S(1)}, s32[1,512]{1,0:T(1,128)}, u32[]{:S(2)}) copy-start(s32[1,512]{1,0:T(1,128)} %param.19) | copy-start | bytes 6148
  7.2 252.9 %copy-start.22 = (f32[64]{0:T(128)S(1)}, f32[64]{0:T(128)}, u32[]{:S(2)}) copy-start(f32[64]{0:T(128)} %param.23) | copy-start | bytes 772
  7.2 256.8 %copy-start.5 = (bf16[1,512,512]{2,1,0:T(8,128)(2,1)S(1)}, bf16[1,512,512]{2,1,0:T(8,128)(2,1)}, u32[]{:S(2)}) copy-start(bf16[1,512,512]{2,1,0:T(8,128)(2,1)} %param.18) | copy-start | bytes 1572868
  7.2 466.0 %reduce-scatter.2.cloned.1.call-start = ((), (), s32[]{:S(2)}) async-start(), calls=%async_computation.1 | async-start | bytes 2703360 | tf_op jit(solution)/shard_map/reduce_scatter | solution.py:288
  8.1 289.2 %collective-permute-start = (bf16[512]{0:T(512)(128)(2,1)S(1)}, bf16[512]{0:T(512)(128)(2,1)}, u32[]{:S(2)}, u32[]{:S(2)}) collective-permute-start(bf16[512]{0:T(512)(128)(2,1)S(1)} %convert_reduce_fusion), channel_id=1, source_target_pairs={{0,1},{1,2},{2,3},{3,4},{4,5},{5,6},{6,7},{7,8},{8,9},{9,10},{10,1... | collective-permute-start | bytes 3080 | tf_op jit(solution)/shard_map/ppermute | solution.py:31
  262.1 41.7 %collective-permute-start.2 = (bf16[512,128]{1,0:T(8,128)(2,1)S(1)}, bf16[512,128]{1,0:T(8,128)(2,1)}, u32[]{:S(2)}, u32[]{:S(2)}) collective-permute-start(bf16[512,128]{1,0:T(8,128)(2,1)S(1)} %pad_maximum_fusion.2), channel_id=1, source_target_pairs={{0,1},{1,2},{2,3},{3,4},{4,5},{5,6},{6,7},{7,8},{8,9},{9,10},{10,1... | collective-permute-start | bytes 393224 | tf_op jit(solution)/shard_map/ppermute | solution.py:31
  264.2 12.2 %copy-start.21 = (f32[4,64]{1,0:T(4,128)S(1)}, f32[4,64]{1,0:T(4,128)}, u32[]{:S(2)}) copy-start(f32[4,64]{1,0:T(4,128)} %param.24) | copy-start | bytes 3076
  270.4 29.5 %collective-permute-start.3 = (bf16[512,512]{1,0:T(8,128)(2,1)}, bf16[512,512]{1,0:T(8,128)(2,1)}, u32[]{:S(2)}, u32[]{:S(2)}) collective-permute-start(bf16[512,512]{1,0:T(8,128)(2,1)} %get-tuple-element.395), channel_id=1, source_target_pairs={{0,1},{1,2},{2,3},{3,4},{4,5},{5,6},{6,7},{7,8},{8,9},{9,10},{10,1... | collective-permute-start | bytes 1572872 | tf_op jit(solution)/shard_map/ppermute | solution.py:31
  274.4 27.4 %collective-permute-start.1 = (bf16[512,512]{1,0:T(8,128)(2,1)}, bf16[512,512]{1,0:T(8,128)(2,1)}, u32[]{:S(2)}, u32[]{:S(2)}) collective-permute-start(bf16[512,512]{1,0:T(8,128)(2,1)} %get-tuple-element.396), channel_id=1, source_target_pairs={{0,1},{1,2},{2,3},{3,4},{4,5},{5,6},{6,7},{7,8},{8,9},{9,10},{10,1... | collective-permute-start | bytes 1572872 | tf_op jit(solution)/shard_map/ppermute | solution.py:31
  329.1 3.2 copy-start.3
  334.6 7.4 %copy-start.7 = (f32[512,4,128]{2,0,1:T(8,128)}, f32[512,4,128]{2,0,1:T(8,128)S(1)}, u32[]{:S(2)}) copy-start(f32[512,4,128]{2,0,1:T(8,128)S(1)} %get-tuple-element.288) | copy-start | bytes 3145732
  334.6 7.4 %copy-start.8 = (f32[512,4,128]{2,0,1:T(8,128)}, f32[512,4,128]{2,0,1:T(8,128)S(1)}, u32[]{:S(2)}) copy-start(f32[512,4,128]{2,0,1:T(8,128)S(1)} %get-tuple-element.284) | copy-start | bytes 3145732
  336.4 40.4 %collective-permute-start.5 = (bf16[512,512]{1,0:T(8,128)(2,1)}, bf16[512,512]{1,0:T(8,128)(2,1)}, u32[]{:S(2)}, u32[]{:S(2)}) collective-permute-start(bf16[512,512]{1,0:T(8,128)(2,1)} %copy_bitcast_fusion.1), channel_id=1, source_target_pairs={{1,0},{2,1},{3,2},{4,3},{5,4},{6,5},{7,6},{8,7},{9,8},{10,9},{11,1... | collective-permute-start | bytes 1572872 | tf_op jit(solution)/shard_map/ppermute | solution.py:31
  340.0 35.2 %collective-permute-start.4 = (bf16[512,512]{1,0:T(8,128)(2,1)}, bf16[512,512]{1,0:T(8,128)(2,1)}, u32[]{:S(2)}, u32[]{:S(2)}) collective-permute-start(bf16[512,512]{1,0:T(8,128)(2,1)} %copy_bitcast_fusion.2), channel_id=1, source_target_pairs={{1,0},{2,1},{3,2},{4,3},{5,4},{6,5},{7,6},{8,7},{9,8},{10,9},{11,1... | collective-permute-start | bytes 1572872 | tf_op jit(solution)/shard_map/ppermute | solution.py:31
  351.1 6.8 %copy-start.4 = (bf16[512,4,128]{0,2,1:T(8,128)(2,1)S(1)}, bf16[512,4,128]{0,2,1:T(8,128)(2,1)}, u32[]{:S(2)}) copy-start(bf16[512,4,128]{0,2,1:T(8,128)(2,1)} %copy.68) | copy-start | bytes 1572868 | tf_op jit(solution)/shard_map/cond
  357.9 8.6 %copy-start.2 = (bf16[512,4,128]{2,1,0:T(4,128)(2,1)S(1)}, bf16[512,4,128]{2,1,0:T(4,128)(2,1)}, u32[]{:S(2)}) copy-start(bf16[512,4,128]{2,1,0:T(4,128)(2,1)} %get-tuple-element.349) | copy-start | bytes 1572868 | tf_op jit(solution)/shard_map/cond
  366.6 3.4 copy-start.1
  373.4 4.9 copy-start.9
  373.4 4.9 copy-start.10
  384.4 82.1 %copy-start.15 = (bf16[512,512]{1,0:T(8,128)(2,1)S(1)}, bf16[512,512]{1,0:T(8,128)(2,1)}, u32[]{:S(2)}) copy-start(bf16[512,512]{1,0:T(8,128)(2,1)} %param.22) | copy-start | bytes 1572868
  384.4 161.2 %all-reduce.7.cloned.1.call-start = ((), (), s32[]{:S(2)}) async-start(), calls=%async_computation.2 | async-start | bytes 163840 | tf_op jit(solution)/shard_map/psum | solution.py:287
  468.8 4.5 copy-start.13
  (8 other events, 15.1 us)
Sparse Core Ops, SparseCore 0:
  384.5 88.4 reduce-scatter.1
  475.3 70.2 all-reduce.6
where the time goes:
time: 559 us; the launch traced here: 555 us
  loops' own time  158 us (28%)
  blocking collectives  94.8 us (17%)
  local copies, waits for them, and re-layouts  80.4 us (14%)
  waiting for transfers between devices  70 us (13%)
  matrix products  61.6 us (11%)
  other arithmetic  54.2 us (10%)
  between operations  20.3 us (4%)
  starting transfers between devices  15.4 us (3%)
    another operation x1, loops' own time, entering(): return lax.fori_loop(0, count - 1, turn, total)  157 us
    psum x1, blocking collectives, body(): grad_mix = lax.psum(grad_mix, ('dp', 'seq'))  79 us
    psum x1, waiting for transfers between devices, body(): lax.psum(jnp.concatenate([proj_part, out_part], 1).astype(jnp.bfloat16),...  69.9 us
    dynamic_slice x62, local copies, waits for them, and re-layouts, turn(): longer = join(total, jax.tree.map(lambda part: part[position], pieces))  39.3 us
    eq x31, other arithmetic, combine(): joined = jnp.where((whole_b == 1) & same, total_a + total_b, total_b)  20.3 us
    unnamed x1, blocking collectives  15.7 us
    ppermute x6, starting transfers between devices, shifted(): return lax.ppermute(array, axis, pairs)  15.4 us
    dot_general x4, matrix products, pair_scores(): jnp.einsum('qhd,khd->hqk', query, keys, preferred_element_type=jnp.float32)  11.3 us
  transfers between devices with their start and end apart: 8, of which 1 were waited for; matrix products, arithmetic and copies ran while one was open for 27% of the time, Pallas kernels for 0%

commit v1 on v0

v1 whole, which is shorter than its diff:
```python
import functools

import jax
import jax.numpy as jnp
from jax import lax
from jax.experimental import pallas as pl
from jax.experimental.pallas import tpu as pltpu
from jax.sharding import PartitionSpec as P

EPS = 1e-05
F32 = jnp.float32
BF = jnp.bfloat16
N = 512
D = 512
H = 4
HD = 128
TQ = 256
WIN = 768
NCH = 5
MESH = pl.DeviceIdType.MESH


def nn(a, b):
    return lax.dot_general(a, b, (((1,), (0,)), ((), ())), preferred_element_type=F32)


def nt(a, b):
    return lax.dot_general(a, b, (((1,), (1,)), ((), ())), preferred_element_type=F32)


def tn(a, b):
    return lax.dot_general(a, b, (((0,), (0,)), ((), ())), preferred_element_type=F32)


def sigmoid(z):
    return 0.5 * jnp.tanh(0.5 * z) + 0.5


def kernel(
    n_dp,
    n_seq,
    x_ref,
    u_ref,
    g_ref,
    w_ref,
    wo_ref,
    f_ref,
    mix_ref,
    cot_ref,
    lo_ref,
    gi_ref,
    gp_out,
    go_out,
    gt_out,
    xprev,
    uprev,
    gprev,
    nrm,
    slope,
    slope_p,
    gate,
    kcat,
    qcat,
    v4,
    maskf,
    cs_own,
    wsav,
    slp,
    att4,
    gated_s,
    ga4,
    dk,
    dv,
    gpa,
    gpq,
    gpg,
    dq4,
    back_s,
    back_r,
    gf,
    s0_s,
    s0_r,
    s1_s,
    s1_r,
    z_r,
    t0_s,
    t0_r,
    t1_r,
    t2_r,
    halo_ss,
    halo_rs,
    back_ss,
    back_rs,
    st_ss,
    st_rs,
    tm_ss,
    tm_rs,
):
    n_yx = n_seq // 2
    rows = D // n_seq
    dp = lax.axis_index("dp")
    s = lax.axis_index("seq")
    core = lax.rem(s, 2)
    m = lax.div(s, 2)
    right = lax.rem(s + 1, n_seq)
    left = lax.rem(s + n_seq - 1, n_seq)
    partner = m * 2 + 1 - core

    def yx_dev(i):
        return (dp, i * 2 + core)

    def z_dev(i):
        return (i, s)

    barrier = pltpu.get_barrier_semaphore()
    for peer in (left, right, partner):
        pl.semaphore_signal(barrier, inc=1, device_id=(dp, peer), device_id_type=MESH)

    @pl.loop(1, n_yx)
    def _(k):
        peer = lax.rem(m + k, n_yx)
        pl.semaphore_signal(barrier, inc=1, device_id=yx_dev(peer), device_id_type=MESH)

    @pl.loop(1, n_dp)
    def _(k):
        peer = lax.rem(dp + k, n_dp)
        pl.semaphore_signal(barrier, inc=1, device_id=z_dev(peer), device_id_type=MESH)

    pl.semaphore_wait(barrier, 3 + (n_yx - 1) + (n_dp - 1))

    def remote(src, dst, ss, rs, dev):
        return pltpu.make_async_remote_copy(
            src_ref=src, dst_ref=dst, send_sem=ss, recv_sem=rs, device_id=dev, device_id_type=MESH
        )

    halo = [
        remote(u_ref, uprev, halo_ss.at[0], halo_rs.at[0], (dp, right)),
        remote(g_ref, gprev, halo_ss.at[1], halo_rs.at[1], (dp, right)),
        remote(x_ref, xprev, halo_ss.at[2], halo_rs.at[2], (dp, right)),
    ]
    for copy in halo:
        copy.start()

    def norm(x):
        wide = x.astype(F32)
        scale = lax.rsqrt(jnp.mean(wide * wide, -1, keepdims=True) + EPS)
        return wide, scale

    wide, scale = norm(x_ref[...])
    nrm[N:, :] = (wide * scale).astype(BF)

    def project(lo, group):
        p = nn(nrm[lo : lo + N, :], w_ref[:, group * D : (group + 1) * D])
        sg = sigmoid(p)
        hid = p * sg
        return hid.astype(BF), sg + hid * (1.0 - sg)

    def put_heads(dst, lo, val):
        for h in range(H):
            dst[h, lo : lo + N, :HD] = val[:, h * HD : (h + 1) * HD]

    hid, sl = project(N, 0)
    gate[...] = hid
    slope[:, 0:D] = sl
    hid, sl = project(N, 1)
    put_heads(v4, N, hid)
    slope[:, D : 2 * D] = sl
    hid, sl = project(N, 2)
    put_heads(qcat, 0, hid)
    slope[:, 2 * D : 3 * D] = sl
    hid, sl = project(N, 3)
    put_heads(kcat, N, hid)
    slope[:, 3 * D : 4 * D] = sl

    halo[0].wait_recv()
    halo[1].wait_recv()
    u_own = u_ref[...].astype(F32)
    u_prev = jnp.where(s == 0, -1.0, uprev[...].astype(F32))
    g_own = g_ref[...].astype(F32)
    g_prev = gprev[...].astype(F32)
    u_all = jnp.concatenate([u_prev, u_own], 1)
    g_all = jnp.broadcast_to(jnp.concatenate([g_prev, g_own], 1), (HD, 2 * N)).astype(BF)
    uc = jnp.transpose(jnp.broadcast_to(u_all, (HD, 2 * N)))[:, :1]
    freq = f_ref[...]
    lane = lax.broadcasted_iota(jnp.int32, (1, HD), 1)

    def features(times):
        ang = times * freq
        return jnp.where(lane < HD // 2, jnp.cos(ang), jnp.sin(ang))

    for a in range(N // TQ):
        q0, k0 = a * TQ, a * TQ
        kpos = lax.broadcasted_iota(jnp.int32, (TQ, WIN), 1) + k0
        qpos = lax.broadcasted_iota(jnp.int32, (TQ, WIN), 0) + (q0 + N)
        same = uc[N + q0 : N + q0 + TQ, :] == u_all[:, k0 : k0 + WIN]
        mk = jnp.where(same & (kpos <= qpos), 1.0, 0.0)
        maskf[q0 : q0 + TQ, :] = mk
        times = nt(mk.astype(BF), g_all[:, k0 : k0 + WIN])
        feat = features(times)
        cs_own[q0 : q0 + TQ, :] = feat
        fb = feat.astype(BF)
        for h in range(H):
            kcat[h, N + q0 : N + q0 + TQ, HD:] = fb
            qcat[h, q0 : q0 + TQ, HD:] = (feat * mix_ref[h : h + 1, :] * (HD**0.5)).astype(BF)
    pi = lax.broadcasted_iota(jnp.int32, (N, N), 0)
    pj = lax.broadcasted_iota(jnp.int32, (N, N), 1)
    mp = jnp.where((uc[:N, :] == u_all[:, :N]) & (pj <= pi), 1.0, 0.0).astype(BF)
    fb = features(nt(mp, g_all[:, :N])).astype(BF)
    for h in range(H):
        kcat[h, :N, HD:] = fb

    halo[2].wait_recv()
    wide, scale = norm(xprev[...])
    nrm[:N, :] = (wide * scale).astype(BF)
    hid, sl = project(0, 1)
    put_heads(v4, 0, hid)
    slope_p[:, :D] = sl
    hid, sl = project(0, 3)
    put_heads(kcat, 0, hid)
    slope_p[:, D:] = sl

    inv = HD**-0.5

    @pl.loop(0, H)
    def _(h):
        for a in range(N // TQ):
            q0, k0 = a * TQ, a * TQ
            z = nt(qcat[h, q0 : q0 + TQ, :], kcat[h, k0 : k0 + WIN, :]) * inv
            sg = sigmoid(z) * maskf[q0 : q0 + TQ, :]
            wt = z * sg
            slp[h, q0 : q0 + TQ, :] = sg + wt * (1.0 - sg)
            wb = wt.astype(BF)
            wsav[h, q0 : q0 + TQ, :] = wb
            att4[h, q0 : q0 + TQ, :] = nn(wb, v4[h, k0 : k0 + WIN, :])

    attended = jnp.concatenate([att4[h] for h in range(H)], 1)
    scale_mid = lax.rsqrt(jnp.mean(attended * attended, -1, keepdims=True) + EPS)
    normed_mid = attended * scale_mid
    gate_wide = gate[...].astype(F32)
    gated = (normed_mid * gate_wide).astype(BF)
    gated_s[...] = gated
    lo_ref[...] = (x_ref[...].astype(F32) + nn(gated, wo_ref[...])).astype(BF)
    grad_gated = nt(cot_ref[...], wo_ref[...])
    gpg[...] = (grad_gated * normed_mid * slope[:, :D]).astype(BF)
    grad_mid = grad_gated * gate_wide
    ga = (
        scale_mid * (grad_mid - normed_mid * jnp.mean(grad_mid * normed_mid, -1, keepdims=True))
    ).astype(BF)
    for h in range(H):
        ga4[h] = ga[:, h * HD : (h + 1) * HD]

    def stage0(c, g):
        g4 = g.reshape(n_yx, 2, rows, D)
        gf[c, 0] = g4[:, 0]
        gf[c, 1] = g4[:, 1]
        s0_s[c] = gf[c, 1 - core].astype(BF)
        remote(s0_s.at[c], s0_r.at[c], st_ss.at[0, c], st_rs.at[0, c], (dp, partner)).start()

    def stage1(c):
        remote(s0_s.at[c], s0_r.at[c], st_ss.at[0, c], st_rs.at[0, c], (dp, partner)).wait_recv()
        s1_s[c] = (gf[c, core] + s0_r[c].astype(F32)).astype(BF)
        s1_r[c, m] = s1_s[c, m]

        @pl.loop(1, n_yx)
        def _(k):
            peer = lax.rem(m + k, n_yx)
            remote(
                s1_s.at[c, peer], s1_r.at[c, m], st_ss.at[1, c], st_rs.at[1, c], yx_dev(peer)
            ).start()

    def wait_all(part, ss, rs, recv):
        copy = remote(part, part, ss, rs, (dp, partner))
        if recv:
            copy.wait_recv()
        else:
            copy.wait_send()

    yx_part = pl.ds(0, n_yx - 1)
    z_part = pl.ds(0, n_dp - 1)

    def stage2(c):
        wait_all(s1_r.at[c, yx_part], st_ss.at[1, c], st_rs.at[1, c], True)
        total = s1_r[c, 0].astype(F32)
        for i in range(1, n_yx):
            total = total + s1_r[c, i].astype(F32)
        z_r[c, dp] = total.astype(BF)

        @pl.loop(1, n_dp)
        def _(k):
            peer = lax.rem(dp + k, n_dp)
            remote(
                z_r.at[c, dp], z_r.at[c, dp], st_ss.at[2, c], st_rs.at[2, c], z_dev(peer)
            ).start()

    factor = float(n_dp * n_seq * N) ** -0.5

    def stage3(c):
        wait_all(z_r.at[c, z_part], st_ss.at[2, c], st_rs.at[2, c], True)
        total = z_r[c, 0].astype(F32)
        for i in range(1, n_dp):
            total = total + z_r[c, i].astype(F32)
        total = total * factor
        if c == 0:
            go_out[...] = total
        else:
            gp_out[:, (c - 1) * D : c * D] = total

    stage0(0, tn(gated_s[...], cot_ref[...]))
    stage0(1, tn(nrm[N:, :], gpg[...]))

    dk[...] = jnp.zeros_like(dk)
    dv[...] = jnp.zeros_like(dv)
    rowid = lax.broadcasted_iota(jnp.int32, (8, HD), 0)

    def head(h, tm):
        for a in range(N // TQ):
            q0, k0 = a * TQ, a * TQ
            gah = ga4[h, q0 : q0 + TQ, :]
            gw = nt(gah, v4[h, k0 : k0 + WIN, :])
            gs = (gw * slp[h, q0 : q0 + TQ, :]).astype(BF)
            dv[h, k0 : k0 + WIN, :] += tn(wsav[h, q0 : q0 + TQ, :], gah)
            dk[h, k0 : k0 + WIN, :] += tn(gs, qcat[h, q0 : q0 + TQ, :HD])
            dqc = nn(gs, kcat[h, k0 : k0 + WIN, :])
            dq4[h, q0 : q0 + TQ, :] = dqc[:, :HD]
            part = jnp.sum(dqc[:, HD:] * cs_own[q0 : q0 + TQ, :], 0, keepdims=True)
            tm = tm + jnp.where(rowid == h, part, 0.0)
        return tm

    tm = lax.fori_loop(0, H, head, jnp.zeros((8, HD), F32))
    t0_s[...] = tm
    tm0 = remote(t0_s, t0_r, tm_ss.at[0], tm_rs.at[0], (dp, partner))
    tm0.start()
    stage1(0)
    stage1(1)

    def join(ref, lo):
        return jnp.concatenate([ref[h, lo : lo + N, :] for h in range(H)], 1)

    gpa[0, :N, :] = (join(dv, 0) * slope_p[:, :D]).astype(BF)
    gpa[1, :N, :] = (join(dk, 0) * (slope_p[:, D:] * inv)).astype(BF)
    back_s[...] = (
        nt(gpa[0, :N, :], w_ref[:, D : 2 * D]) + nt(gpa[1, :N, :], w_ref[:, 3 * D :])
    ).astype(BF)
    back = remote(back_s, back_r, back_ss.at[0], back_rs.at[0], (dp, left))
    back.start()
    gpa[0, N:, :] = (join(dv, N) * slope[:, D : 2 * D]).astype(BF)
    gpa[1, N:, :] = (join(dk, N) * (slope[:, 3 * D :] * inv)).astype(BF)
    gpq[...] = (join(dq4, 0) * (slope[:, 2 * D : 3 * D] * inv)).astype(BF)
    stage0(2, tn(nrm[...], gpa[0]))
    stage0(3, tn(nrm[N:, :], gpq[...]))
    stage2(0)
    stage2(1)
    stage0(4, tn(nrm[...], gpa[1]))

    tm0.wait_recv()
    t1_r[m] = t0_s[...] + t0_r[...]

    @pl.loop(1, n_yx)
    def _(k):
        peer = lax.rem(m + k, n_yx)
        remote(t1_r.at[m], t1_r.at[m], tm_ss.at[1], tm_rs.at[1], yx_dev(peer)).start()

    stage1(2)
    stage1(3)
    stage1(4)
    gn = (
        nt(gpg[...], w_ref[:, :D])
        + nt(gpa[0, N:, :], w_ref[:, D : 2 * D])
        + nt(gpq[...], w_ref[:, 2 * D : 3 * D])
        + nt(gpa[1, N:, :], w_ref[:, 3 * D :])
    )
    wide, scale = norm(x_ref[...])
    unit = wide * scale
    stage2(2)
    stage2(3)
    stage2(4)
    wait_all(t1_r.at[yx_part], tm_ss.at[1], tm_rs.at[1], True)
    tsum = t1_r[0]
    for i in range(1, n_yx):
        tsum = tsum + t1_r[i]
    t2_r[dp] = tsum

    @pl.loop(1, n_dp)
    def _(k):
        peer = lax.rem(dp + k, n_dp)
        remote(t2_r.at[dp], t2_r.at[dp], tm_ss.at[2], tm_rs.at[2], z_dev(peer)).start()

    back.wait_recv()
    gn = gn + back_r[...].astype(F32)
    gi_ref[...] = (
        cot_ref[...].astype(F32) + scale * (gn - unit * jnp.mean(gn * unit, -1, keepdims=True))
    ).astype(BF)
    for c in range(NCH):
        stage3(c)
    wait_all(t2_r.at[z_part], tm_ss.at[2], tm_rs.at[2], True)
    tsum = t2_r[0]
    for i in range(1, n_dp):
        tsum = tsum + t2_r[i]
    tsum = (tsum + pltpu.roll(tsum, HD // 2, 1)) * factor
    gt_out[...] = tsum[:H, : HD // 2]

    for copy in halo:
        copy.wait_send()
    back.wait_send()
    tm0.wait_send()
    for c in range(NCH):
        remote(s0_s.at[c], s0_r.at[c], st_ss.at[0, c], st_rs.at[0, c], (dp, partner)).wait_send()
        wait_all(s1_r.at[c, yx_part], st_ss.at[1, c], st_rs.at[1, c], False)
        wait_all(z_r.at[c, z_part], st_ss.at[2, c], st_rs.at[2, c], False)
    wait_all(t1_r.at[yx_part], tm_ss.at[1], tm_rs.at[1], False)
    wait_all(t2_r.at[z_part], tm_ss.at[2], tm_rs.at[2], False)


def body(n_dp, n_seq, embeddings, user_ids, time_gaps, proj, out_w, freqs, mix, cot):
    n_yx = n_seq // 2
    rows = D // n_seq
    freq2 = jnp.concatenate([freqs, freqs])[None]
    mix2 = jnp.concatenate([mix, mix], 1)
    vm = pltpu.VMEM
    dma = pltpu.SemaphoreType.DMA
    scratch = [
        vm((N, D), BF),
        vm((1, N), jnp.int32),
        vm((1, N), jnp.int32),
        vm((2 * N, D), BF),
        vm((N, 4 * D), F32),
        vm((N, 2 * D), F32),
        vm((N, D), BF),
        vm((H, 2 * N, 2 * HD), BF),
        vm((H, N, 2 * HD), BF),
        vm((H, 2 * N, HD), BF),
        vm((N, WIN), F32),
        vm((N, HD), F32),
        vm((H, N, WIN), BF),
        vm((H, N, WIN), F32),
        vm((H, N, HD), F32),
        vm((N, D), BF),
        vm((H, N, HD), BF),
        vm((H, 2 * N, HD), F32),
        vm((H, 2 * N, HD), F32),
        vm((2, 2 * N, D), BF),
        vm((N, D), BF),
        vm((N, D), BF),
        vm((H, N, HD), F32),
        vm((N, D), BF),
        vm((N, D), BF),
        vm((NCH, 2, n_yx, rows, D), F32),
        vm((NCH, n_yx, rows, D), BF),
        vm((NCH, n_yx, rows, D), BF),
        vm((NCH, n_yx, rows, D), BF),
        vm((NCH, n_yx, rows, D), BF),
        vm((NCH, n_dp, rows, D), BF),
        vm((8, HD), F32),
        vm((8, HD), F32),
        vm((n_yx, 8, HD), F32),
        vm((n_dp, 8, HD), F32),
        dma((3,)),
        dma((3,)),
        dma((1,)),
        dma((1,)),
        dma((3, NCH)),
        dma((3, NCH)),
        dma((3,)),
        dma((3,)),
    ]
    spec = pl.BlockSpec(memory_space=pltpu.VMEM)
    lo, gi, gp, go, gt = pl.pallas_call(
        functools.partial(kernel, n_dp, n_seq),
        out_shape=(
            jax.ShapeDtypeStruct((N, D), BF),
            jax.ShapeDtypeStruct((N, D), BF),
            jax.ShapeDtypeStruct((rows, 4 * D), F32),
            jax.ShapeDtypeStruct((rows, D), F32),
            jax.ShapeDtypeStruct((H, HD // 2), F32),
        ),
        in_specs=[spec] * 8,
        out_specs=(spec,) * 5,
        scratch_shapes=scratch,
        compiler_params=pltpu.CompilerParams(
            collective_id=0, has_side_effects=True, vmem_limit_bytes=62 * 1024 * 1024
        ),
        name="layer",
    )(embeddings[0], user_ids, time_gaps, proj, out_w, freq2, mix2, cot[0])
    return lo[None], gi[None], gp, go, gt


def solution(mesh):
    n_dp, n_seq = mesh.shape["dp"], mesh.shape["seq"]
    return jax.shard_map(
        functools.partial(body, n_dp, n_seq),
        mesh=mesh,
        in_specs=(
            P("dp", "seq", None),
            P("dp", "seq"),
            P("dp", "seq"),
            P(),
            P(),
            P(),
            P(),
            P("dp", "seq", None),
        ),
        out_specs=(P("dp", "seq", None), P("dp", "seq", None), P("seq", None), P("seq", None), P()),
        check_vma=False,
    )
```

time: 559 us -> 69.7 us (0.12)
  loops' own time: 158 us -> 0 us
  blocking collectives: 94.8 us -> 0 us
  local copies, waits for them, and re-layouts: 80.4 us -> 5.64 us
  waiting for transfers between devices: 70 us -> 0 us
  matrix products: 61.6 us -> 0 us
  Pallas kernels: 0 us -> 60.5 us
  other arithmetic: 54.2 us -> 2.72 us
  between operations: 20.3 us -> 0.67 us
  starting transfers between devices: 15.4 us -> 0 us
    another operation x5 -> x0, loops' own time: 158 us -> none  [the longest x1 157 us: entering(): return lax.fori_loop(0, count - 1, turn, total)]
    psum x1 -> x0, blocking collectives: 79 us -> none  [body(): grad_mix = lax.psum(grad_mix, ('dp', 'seq'))]
    psum x1 -> x0, waiting for transfers between devices: 69.9 us -> none  [body(): lax.psum(jnp.concatenate([proj_part, out_part], 1).astype(jnp.bfloat16),...]
    dot_general x24 -> x0, matrix products: 61.6 us -> none  [the longest x4 11.3 us: pair_scores(): jnp.einsum('qhd,khd->hqk', query, keys, preferred_element_type=jnp.float32)]
    pallas_call x0 -> x1, Pallas kernels: none -> 60.5 us  [body(): pl.pallas_call(functools.partial(kernel, n_dp, n_seq), out_shape=(jax.Sha...]
    dynamic_slice x62 -> x0, local copies, waits for them, and re-layouts: 39.3 us -> none  [turn(): longer = join(total, jax.tree.map(lambda part: part[position], pieces))]
    eq x31 -> x0, other arithmetic: 20.3 us -> none  [combine(): joined = jnp.where((whole_b == 1) & same, total_a + total_b, total_b)]
    unnamed x1 -> x0, blocking collectives: 15.7 us -> none
  transfers between devices with their start and end apart: 8 -> 0, of which waited for: 1 -> 0; matrix products, arithmetic and copies ran while one was open for 27% -> 0% of each run, Pallas kernels for 0% -> 0%
where the time goes in v1:
time: 69.7 us; the launch traced here: 69.5 us
  Pallas kernels  60.5 us (87%)
  local copies, waits for them, and re-layouts  5.64 us (8%)
  other arithmetic  2.72 us (4%)
    pallas_call x1, Pallas kernels, body(): pl.pallas_call(functools.partial(kernel, n_dp, n_seq), out_shape=(jax.Sha...  60.5 us
    unnamed x11, local copies, waits for them, and re-layouts  5.64 us
    concatenate x1, other arithmetic, body(): mix2 = jnp.concatenate([mix, mix], 1)  1.41 us

profile of v1, /device:TPU:6, one launch (start us, length us, event | category | flops | bytes accessed | tf_op | source)
XLA Modules:
  0.0 69.5 jit_solution(7443243217030267421)
XLA Ops:
  0.6 1.3 %maximum_bitcast_fusion.f_ref = f32[1,128]{1,0:T(1,128)} fusion(f32[64]{0:T(128)} %param.13), kind=kLoop, calls=%fused_computation.1 | loop fusion | flops 128 | bytes 768 | tf_op jit(solution)/shard_map/broadcast_in_dim | solution.py:417
  1.9 1.4 %pad_maximum_fusion.mix_ref = f32[4,128]{1,0:T(4,128)} fusion(f32[4,64]{1,0:T(4,128)} %param.14), kind=kLoop, calls=%fused_computation | loop fusion | flops 512 | bytes 3072 | tf_op jit(solution)/shard_map/concatenate | solution.py:418
  3.4 60.5 %layer.1 = (bf16[512,512]{1,0:T(8,128)(2,1)}, bf16[512,512]{1,0:T(8,128)(2,1)}, f32[16,2048]{1,0:T(8,128)}, f32[16,512]{1,0:T(8,128)}, f32[4,64]{1,0:T(4,128)}) custom-call(bf16[512,512]{1,0:T(8,128)(2,1)} %bitcast.8, s32[1,512]{1,0:T(1,128)} %u_ref.1, s32[1,512]{1,0:T(1,128)} %g_ref.1, bf16[512,2048]{1,0:T(8,128)(2,1)} %w_ref.1, bf16[512,512]{1,0:T(8,128)(2,1)} %wo_ref.1, ...), custom_call_target="tpu_custom_call" | custom-call | tf_op jit(solution)/shard_map/layer/pallas_call | solution.py:467
  63.8 0.0 copy-start
  63.8 0.0 copy-start.1
  63.8 0.0 copy-start.2
  63.9 1.9 %copy.18 = bf16[1,512,512]{2,1,0:T(8,128)(2,1)} copy(bf16[1,512,512]{2,1,0:T(8,128)(2,1)} %bitcast.7) | data formatting | bytes 1048576
  65.8 1.9 %copy.19 = bf16[1,512,512]{2,1,0:T(8,128)(2,1)} copy(bf16[1,512,512]{2,1,0:T(8,128)(2,1)} %bitcast.6) | data formatting | bytes 1048576
  67.6 0.0 copy-done
  67.6 0.7 copy.20
  68.3 0.0 copy-done.1
  68.3 0.6 copy.21
  68.9 0.0 copy-done.2
  68.9 0.6 copy.22
Async XLA Ops:
  63.8 3.8 %copy-start = (f32[16,2048]{1,0:T(8,128)S(1)}, f32[16,2048]{1,0:T(8,128)}, u32[]{:S(2)}) copy-start(f32[16,2048]{1,0:T(8,128)} %get-tuple-element.22) | copy-start | bytes 393220
  63.8 4.5 %copy-start.1 = (f32[16,512]{1,0:T(8,128)S(1)}, f32[16,512]{1,0:T(8,128)}, u32[]{:S(2)}) copy-start(f32[16,512]{1,0:T(8,128)} %get-tuple-element.23) | copy-start | bytes 98308
  63.8 5.1 %copy-start.2 = (f32[4,64]{1,0:T(4,128)S(1)}, f32[4,64]{1,0:T(4,128)}, u32[]{:S(2)}) copy-start(f32[4,64]{1,0:T(4,128)} %get-tuple-element.24) | copy-start | bytes 3076

commit v2 on v1

v2 whole, which is shorter than its diff:
```python
import functools

import jax
import jax.numpy as jnp
from jax import lax
from jax.experimental import pallas as pl
from jax.experimental.pallas import tpu as pltpu
from jax.sharding import PartitionSpec as P

EPS = 1e-05
F32 = jnp.float32
BF = jnp.bfloat16
N = 512
D = 512
H = 4
HD = 128
TQ = 256
WIN = 768
MESH = pl.DeviceIdType.MESH


def nn(a, b):
    return lax.dot_general(a, b, (((1,), (0,)), ((), ())), preferred_element_type=F32)


def nt(a, b):
    return lax.dot_general(a, b, (((1,), (1,)), ((), ())), preferred_element_type=F32)


def tn(a, b):
    return lax.dot_general(a, b, (((0,), (0,)), ((), ())), preferred_element_type=F32)


def sigmoid(z):
    return 0.5 * jnp.tanh(0.5 * z) + 0.5


COS = (1.0, -1 / 2, 1 / 24, -1 / 720, 1 / 40320, -1 / 3628800, 1 / 479001600)
PI_PARTS = (3.140625, 9.67502593994140625e-4, 1.509957990978376432e-7)


def cos_sin(ang, half):
    k = jnp.floor(ang * (1.0 / 3.141592653589793) - half + 0.5)
    c = k + half
    r = ((ang - c * PI_PARTS[0]) - c * PI_PARTS[1]) - c * PI_PARTS[2]
    r2 = r * r
    p = jnp.full_like(r2, COS[-1])
    for q in COS[-2::-1]:
        p = p * r2 + q
    odd = k * 0.5
    odd = odd - jnp.floor(odd)
    return p * (1.0 - 4.0 * odd)


def kernel(n_dp, n_seq, names, *refs):
    r = dict(zip(names, refs))
    x_ref, u_ref, g_ref, w_ref, wo_ref, f_ref, mix_ref, cot_ref = refs[:8]
    lo_ref, gi_ref, gp_out, go_out, gt_out = refs[8:13]
    xv, xp, wv, wov, cotv = r["xv"], r["xp"], r["wv"], r["wov"], r["cotv"]
    uprev, gprev = r["uprev"], r["gprev"]
    nrm, nrmt, gatt = r["nrm"], r["nrmt"], r["gatt"]
    sl_v, sl_k, sl_q, sl_g = r["sl_v"], r["sl_k"], r["sl_q"], r["sl_g"]
    gate, kcat, qcat, v4 = r["gate"], r["kcat"], r["qcat"], r["v4"]
    maskf, cs_own, wsav, slp, att4 = r["maskf"], r["cs_own"], r["wsav"], r["slp"], r["att4"]
    ggs, ga4, gpv, gpk, gpq, gpg = r["ggs"], r["ga4"], r["gpv"], r["gpk"], r["gpq"], r["gpg"]
    back_s, back_r = r["back_s"], r["back_r"]
    t0_s, t0_r, t1_r, t2_r = r["t0_s"], r["t0_r"], r["t1_r"], r["t2_r"]
    in_sem, halo_ss, halo_rs = r["in_sem"], r["halo_ss"], r["halo_rs"]
    back_ss, back_rs, tm_ss, tm_rs = r["back_ss"], r["back_rs"], r["tm_ss"], r["tm_rs"]

    n_yx = n_seq // 2
    rows = D // n_seq
    half = D // 2
    dp = lax.axis_index("dp")
    s = lax.axis_index("seq")
    core = lax.rem(s, 2)
    m = lax.div(s, 2)
    right = lax.rem(s + 1, n_seq)
    left = lax.rem(s + n_seq - 1, n_seq)
    partner = m * 2 + 1 - core

    def yx_dev(i):
        return (dp, i * 2 + core)

    def z_dev(i):
        return (i, s)

    barrier = pltpu.get_barrier_semaphore()
    for peer in (left, right, partner):
        pl.semaphore_signal(barrier, inc=1, device_id=(dp, peer), device_id_type=MESH)

    @pl.loop(1, n_yx)
    def _(k):
        peer = lax.rem(m + k, n_yx)
        pl.semaphore_signal(barrier, inc=1, device_id=yx_dev(peer), device_id_type=MESH)

    @pl.loop(1, n_dp)
    def _(k):
        peer = lax.rem(dp + k, n_dp)
        pl.semaphore_signal(barrier, inc=1, device_id=z_dev(peer), device_id_type=MESH)

    loads = [
        pltpu.make_async_copy(x_ref, xv, in_sem.at[0]),
        pltpu.make_async_copy(w_ref, wv, in_sem.at[1]),
        pltpu.make_async_copy(wo_ref, wov, in_sem.at[2]),
        pltpu.make_async_copy(cot_ref, cotv, in_sem.at[3]),
    ]
    for copy in loads:
        copy.start()

    def remote(src, dst, ss, rs, dev):
        return pltpu.make_async_remote_copy(
            src_ref=src, dst_ref=dst, send_sem=ss, recv_sem=rs, device_id=dev, device_id_type=MESH
        )

    hi, lo = pl.ds(TQ, TQ), pl.ds(0, TQ)
    halo = [
        remote(u_ref, uprev, halo_ss.at[0], halo_rs.at[0], (dp, right)),
        remote(g_ref, gprev, halo_ss.at[1], halo_rs.at[1], (dp, right)),
        remote(xv.at[hi], xp.at[hi], halo_ss.at[2], halo_rs.at[2], (dp, right)),
        remote(xv.at[lo], xp.at[lo], halo_ss.at[3], halo_rs.at[3], (dp, right)),
    ]

    def norm(x):
        wide = x.astype(F32)
        scale = lax.rsqrt(jnp.mean(wide * wide, -1, keepdims=True) + EPS)
        return wide, scale

    def project(at, n, group):
        p = nn(nrm[at : at + n, :], wv[:, group * D : (group + 1) * D])
        sg = sigmoid(p)
        hid = p * sg
        return hid.astype(BF), sg + hid * (1.0 - sg)

    def put_heads(dst, at, val):
        n = val.shape[0]
        for h in range(H):
            dst[h, at : at + n, :HD] = val[:, h * HD : (h + 1) * HD]

    def put_kv(at, n):
        hid, sl = project(at, n, 1)
        put_heads(v4, at, hid)
        sl_v[at : at + n, :] = sl
        hid, sl = project(at, n, 3)
        put_heads(kcat, at, hid)
        sl_k[at : at + n, :] = sl

    def put_nrmt(at, n):
        t4 = jnp.transpose(nrm[at : at + n, :]).reshape(n_yx, 2, rows, n)
        for c in range(2):
            nrmt[c, :, at : at + n] = t4[:, c].reshape(half, n)

    loads[0].wait()
    wide, scale = norm(xv[...])
    nrm[N:, :] = (wide * scale).astype(BF)
    loads[1].wait()
    hid, sl = project(N, N, 0)
    gate[...] = hid
    sl_g[...] = sl

    pl.semaphore_wait(barrier, 3 + (n_yx - 1) + (n_dp - 1))
    for copy in halo:
        copy.start()

    put_kv(N, N)
    hid, sl = project(N, N, 2)
    put_heads(qcat, 0, hid)
    sl_q[...] = sl
    put_nrmt(N, N)
    loads[2].wait()
    loads[3].wait()
    ggs[...] = nt(cotv[...], wov[...])

    halo[0].wait_recv()
    halo[1].wait_recv()
    u_own = u_ref[...].astype(F32)
    u_prev = jnp.where(s == 0, -1.0, uprev[...].astype(F32))
    g_own = g_ref[...].astype(F32)
    g_prev = gprev[...].astype(F32)
    u_all = jnp.concatenate([u_prev, u_own], 1)
    g_all = jnp.broadcast_to(jnp.concatenate([g_prev, g_own], 1), (HD, 2 * N)).astype(BF)
    uc = jnp.transpose(jnp.broadcast_to(u_all, (HD, 2 * N)))[:, :1]
    freq = jnp.concatenate([f_ref[...], f_ref[...]], 1)
    mix = jnp.concatenate([mix_ref[...], mix_ref[...]], 1) * (HD**0.5)
    lane = lax.broadcasted_iota(jnp.int32, (1, HD), 1)
    shift = jnp.where(lane < HD // 2, 0.0, 0.5)

    def features(times):
        return cos_sin(times * freq, shift)

    for a in range(N // TQ):
        q0, k0 = a * TQ, a * TQ
        kpos = lax.broadcasted_iota(jnp.int32, (TQ, WIN), 1) + k0
        qpos = lax.broadcasted_iota(jnp.int32, (TQ, WIN), 0) + (q0 + N)
        same = uc[N + q0 : N + q0 + TQ, :] == u_all[:, k0 : k0 + WIN]
        mk = jnp.where(same & (kpos <= qpos), 1.0, 0.0)
        maskf[q0 : q0 + TQ, :] = mk
        feat = features(nt(mk.astype(BF), g_all[:, k0 : k0 + WIN]))
        cs_own[q0 : q0 + TQ, :] = feat
        fb = feat.astype(BF)
        for h in range(H):
            kcat[h, N + q0 : N + q0 + TQ, HD:] = fb
            qcat[h, q0 : q0 + TQ, HD:] = (feat * mix[h : h + 1, :]).astype(BF)
    pi = lax.broadcasted_iota(jnp.int32, (N, N), 0)
    pj = lax.broadcasted_iota(jnp.int32, (N, N), 1)
    mp = jnp.where((uc[:N, :] == u_all[:, :N]) & (pj <= pi), 1.0, 0.0).astype(BF)
    fb = features(nt(mp, g_all[:, :N])).astype(BF)
    for h in range(H):
        kcat[h, :N, HD:] = fb

    inv = HD**-0.5

    def piece(h, a, col, n):
        q0 = a * TQ
        k0 = q0 + col
        z = nt(qcat[h, q0 : q0 + TQ, :], kcat[h, k0 : k0 + n, :]) * inv
        sg = sigmoid(z) * maskf[q0 : q0 + TQ, col : col + n]
        wt = z * sg
        slp[h, q0 : q0 + TQ, col : col + n] = sg + wt * (1.0 - sg)
        wb = wt.astype(BF)
        wsav[h, q0 : q0 + TQ, col : col + n] = wb
        return nn(wb, v4[h, k0 : k0 + n, :])

    @pl.loop(0, H)
    def _(h):
        att4[h, :TQ, :] = piece(h, 0, N, TQ)
        att4[h, TQ:, :] = piece(h, 1, TQ, N)

    def halo_norm(at):
        wide, scale = norm(xp[at : at + TQ, :])
        nrm[at : at + TQ, :] = (wide * scale).astype(BF)
        put_kv(at, TQ)

    halo[2].wait_recv()
    halo_norm(TQ)

    @pl.loop(0, H)
    def _(h):
        att4[h, :TQ, :] += piece(h, 0, TQ, TQ)
        att4[h, TQ:, :] += piece(h, 1, 0, TQ)

    halo[3].wait_recv()
    halo_norm(0)

    @pl.loop(0, H)
    def _(h):
        att4[h, :TQ, :] += piece(h, 0, 0, TQ)

    attended = jnp.concatenate([att4[h] for h in range(H)], 1)
    scale_mid = lax.rsqrt(jnp.mean(attended * attended, -1, keepdims=True) + EPS)
    normed_mid = attended * scale_mid
    gate_wide = gate[...].astype(F32)
    gated = (normed_mid * gate_wide).astype(BF)
    t4 = jnp.transpose(gated).reshape(n_yx, 2, rows, N)
    for c in range(2):
        gatt[c] = t4[:, c].reshape(half, N)
    grad_gated = ggs[...]
    gpg[...] = (grad_gated * normed_mid * sl_g[...]).astype(BF)
    grad_mid = grad_gated * gate_wide
    ga = (
        scale_mid * (grad_mid - normed_mid * jnp.mean(grad_mid * normed_mid, -1, keepdims=True))
    ).astype(BF)
    for h in range(H):
        ga4[h] = ga[:, h * HD : (h + 1) * HD]

    def part(name, c):
        return r[c[0] + name].at[c[1]]

    def part_sem(name, c):
        i = c[1] + (0 if c[0] == "o" else 2)
        return lambda stage: r[name].at[stage, i]

    def stage_copy(stage, c, src, dst, dev):
        return remote(src, dst, part_sem("st_ss", c)(stage), part_sem("st_rs", c)(stage), dev)

    def s0_copy(c):
        return stage_copy(0, c, part("s0_s", c), part("s0_r", c), (dp, partner))

    def stage0(c, grad):
        width = 512 if c[0] == "o" else 3 * HD
        part("s0_s", c)[...] = grad(1 - core).reshape(n_yx, rows, width).astype(BF)
        s0_copy(c).start()
        part("own", c)[...] = grad(core).reshape(n_yx, rows, width)

    def stage1(c):
        s0_copy(c).wait_recv()
        s1_s, s1_r = part("s1_s", c), part("s1_r", c)
        s1_s[...] = (part("own", c)[...] + part("s0_r", c)[...].astype(F32)).astype(BF)
        s1_r[m] = s1_s[m]

        @pl.loop(1, n_yx)
        def _(k):
            peer = lax.rem(m + k, n_yx)
            stage_copy(1, c, s1_s.at[peer], s1_r.at[m], yx_dev(peer)).start()

    yx_part = pl.ds(0, n_yx - 1)
    z_part = pl.ds(0, n_dp - 1)

    def s1_all(c):
        ref = part("s1_r", c).at[yx_part]
        return stage_copy(1, c, ref, ref, (dp, partner))

    def z_all(c):
        ref = part("z_r", c).at[z_part]
        return stage_copy(2, c, ref, ref, (dp, partner))

    def stage2(c):
        s1_all(c).wait_recv()
        s1_r, z_r = part("s1_r", c), part("z_r", c)
        total = s1_r[0].astype(F32)
        for i in range(1, n_yx):
            total = total + s1_r[i].astype(F32)
        z_r[dp] = total.astype(BF)

        @pl.loop(1, n_dp)
        def _(k):
            peer = lax.rem(dp + k, n_dp)
            stage_copy(2, c, z_r.at[dp], z_r.at[dp], z_dev(peer)).start()

    factor = float(n_dp * n_seq * N) ** -0.5

    def stage3(c):
        z_all(c).wait_recv()
        z_r = part("z_r", c)
        total = z_r[0].astype(F32)
        for i in range(1, n_dp):
            total = total + z_r[i].astype(F32)
        total = total * factor
        if c == ("o", 0):
            go_out[...] = total
        elif c == ("o", 1):
            gp_out[:, :D] = total
        else:
            for i in range(3):
                at = (1 + i) * D + c[1] * HD
                gp_out[:, at : at + HD] = total[:, i * HD : (i + 1) * HD]

    out_c, gate_c = ("o", 0), ("o", 1)
    stage0(out_c, lambda c: nn(gatt[c], cotv[...]))
    stage0(gate_c, lambda c: nn(nrmt[c, :, N:], gpg[...]))
    put_nrmt(0, N)
    lo_ref[...] = (xv[...].astype(F32) + nn(gated, wov[...])).astype(BF)

    rowid = lax.broadcasted_iota(jnp.int32, (8, HD), 0)

    def head(h, tm):
        cols = slice(h * HD, (h + 1) * HD)
        tv, tk = [], []
        for a in range(N // TQ):
            q0, k0 = a * TQ, a * TQ
            gah = ga4[h, q0 : q0 + TQ, :]
            gw = nt(gah, v4[h, k0 : k0 + WIN, :])
            gs = (gw * slp[h, q0 : q0 + TQ, :]).astype(BF)
            tv.append(tn(wsav[h, q0 : q0 + TQ, :], gah))
            tk.append(tn(gs, qcat[h, q0 : q0 + TQ, :HD]))
            dqc = nn(gs, kcat[h, k0 : k0 + WIN, :])
            gpq[q0 : q0 + TQ, cols] = (dqc[:, :HD] * (sl_q[q0 : q0 + TQ, cols] * inv)).astype(BF)
            got = jnp.sum(dqc[:, HD:] * cs_own[q0 : q0 + TQ, :], 0, keepdims=True)
            tm = tm + jnp.where(rowid == h, got, 0.0)
        for dst, t, sl, f in ((gpv, tv, sl_v, 1.0), (gpk, tk, sl_k, inv)):
            dst[:TQ, cols] = (t[0][:TQ] * (sl[:TQ, cols] * f)).astype(BF)
            dst[TQ:WIN, cols] = ((t[0][TQ:] + t[1][:N]) * (sl[TQ:WIN, cols] * f)).astype(BF)
            dst[WIN:, cols] = (t[1][N:] * (sl[WIN:, cols] * f)).astype(BF)
        return tm

    def head_grad(h):
        cols = slice(h * HD, (h + 1) * HD)

        def grad(c):
            vk = nn(nrmt[c], jnp.concatenate([gpv[:, cols], gpk[:, cols]], 1))
            q = nn(nrmt[c, :, N:], gpq[:, cols])
            return jnp.concatenate([vk[:, :HD], q, vk[:, HD:]], 1)

        return grad

    hc = [("h", h) for h in range(H)]
    tm = head(0, jnp.zeros((8, HD), F32))
    stage1(out_c)
    stage0(hc[0], head_grad(0))
    tm = head(1, tm)
    stage1(gate_c)
    stage1(hc[0])
    stage0(hc[1], head_grad(1))
    tm = head(2, tm)
    stage1(hc[1])
    stage2(out_c)
    stage0(hc[2], head_grad(2))
    tm = head(3, tm)
    stage1(hc[2])
    stage2(gate_c)
    t0_s[...] = tm
    tm0 = remote(t0_s, t0_r, tm_ss.at[0], tm_rs.at[0], (dp, partner))
    tm0.start()
    stage0(hc[3], head_grad(3))
    back_s[...] = (nt(gpv[:N, :], wv[:, D : 2 * D]) + nt(gpk[:N, :], wv[:, 3 * D :])).astype(BF)
    stage2(hc[0])
    tm0.wait_recv()
    t1_r[m] = t0_s[...] + t0_r[...]

    @pl.loop(1, n_yx)
    def _(k):
        peer = lax.rem(m + k, n_yx)
        remote(t1_r.at[m], t1_r.at[m], tm_ss.at[1], tm_rs.at[1], yx_dev(peer)).start()

    stage1(hc[3])
    back = remote(back_s, back_r, back_ss.at[0], back_rs.at[0], (dp, left))
    back.start()
    stage2(hc[1])
    gn = (
        nt(gpg[...], wv[:, :D])
        + nt(gpv[N:, :], wv[:, D : 2 * D])
        + nt(gpq[...], wv[:, 2 * D : 3 * D])
        + nt(gpk[N:, :], wv[:, 3 * D :])
    )
    ggs[...] = gn

    def tm_all(ref, i):
        return remote(ref, ref, tm_ss.at[i], tm_rs.at[i], (dp, partner))

    tm1, tm2 = tm_all(t1_r.at[yx_part], 1), tm_all(t2_r.at[z_part], 2)
    tm1.wait_recv()
    tsum = t1_r[0]
    for i in range(1, n_yx):
        tsum = tsum + t1_r[i]
    t2_r[dp] = tsum

    @pl.loop(1, n_dp)
    def _(k):
        peer = lax.rem(dp + k, n_dp)
        remote(t2_r.at[dp], t2_r.at[dp], tm_ss.at[2], tm_rs.at[2], z_dev(peer)).start()

    stage2(hc[2])
    stage3(out_c)
    stage3(gate_c)
    stage2(hc[3])
    stage3(hc[0])
    back.wait_recv()
    wide, scale = norm(xv[...])
    unit = wide * scale
    gn = ggs[...] + back_r[...].astype(F32)
    gi_ref[...] = (
        cotv[...].astype(F32) + scale * (gn - unit * jnp.mean(gn * unit, -1, keepdims=True))
    ).astype(BF)
    stage3(hc[1])
    stage3(hc[2])
    tm2.wait_recv()
    tsum = t2_r[0]
    for i in range(1, n_dp):
        tsum = tsum + t2_r[i]
    tsum = (tsum + pltpu.roll(tsum, HD // 2, 1)) * factor
    gt_out[...] = tsum[:H, : HD // 2]
    stage3(hc[3])

    for copy in halo:
        copy.wait_send()
    back.wait_send()
    tm0.wait_send()
    tm1.wait_send()
    tm2.wait_send()
    for c in [out_c, gate_c] + hc:
        s0_copy(c).wait_send()
        s1_all(c).wait_send()
        z_all(c).wait_send()


def body(n_dp, n_seq, embeddings, user_ids, time_gaps, proj, out_w, freqs, mix, cot):
    n_yx = n_seq // 2
    rows = D // n_seq
    vm = pltpu.VMEM
    dma = pltpu.SemaphoreType.DMA
    scratch = {
        "xv": vm((N, D), BF),
        "xp": vm((N, D), BF),
        "wv": vm((D, 4 * D), BF),
        "wov": vm((D, D), BF),
        "cotv": vm((N, D), BF),
        "uprev": vm((1, N), jnp.int32),
        "gprev": vm((1, N), jnp.int32),
        "nrm": vm((2 * N, D), BF),
        "nrmt": vm((2, D // 2, 2 * N), BF),
        "gatt": vm((2, D // 2, N), BF),
        "sl_v": vm((2 * N, D), F32),
        "sl_k": vm((2 * N, D), F32),
        "sl_q": vm((N, D), F32),
        "sl_g": vm((N, D), F32),
        "gate": vm((N, D), BF),
        "kcat": vm((H, 2 * N, 2 * HD), BF),
        "qcat": vm((H, N, 2 * HD), BF),
        "v4": vm((H, 2 * N, HD), BF),
        "maskf": vm((N, WIN), F32),
        "cs_own": vm((N, HD), F32),
        "wsav": vm((H, N, WIN), BF),
        "slp": vm((H, N, WIN), F32),
        "att4": vm((H, N, HD), F32),
        "ggs": vm((N, D), F32),
        "ga4": vm((H, N, HD), BF),
        "gpv": vm((2 * N, D), BF),
        "gpk": vm((2 * N, D), BF),
        "gpq": vm((N, D), BF),
        "gpg": vm((N, D), BF),
        "back_s": vm((N, D), BF),
        "back_r": vm((N, D), BF),
        "t0_s": vm((8, HD), F32),
        "t0_r": vm((8, HD), F32),
        "t1_r": vm((n_yx, 8, HD), F32),
        "t2_r": vm((n_dp, 8, HD), F32),
        "in_sem": dma((4,)),
        "halo_ss": dma((4,)),
        "halo_rs": dma((4,)),
        "back_ss": dma((1,)),
        "back_rs": dma((1,)),
        "st_ss": dma((3, 2 + H)),
        "st_rs": dma((3, 2 + H)),
        "tm_ss": dma((3,)),
        "tm_rs": dma((3,)),
    }
    for kind, count, width in (("o", 2, D), ("h", H, 3 * HD)):
        for name in ("s0_s", "s0_r", "s1_s", "s1_r"):
            scratch[kind + name] = vm((count, n_yx, rows, width), BF)
        scratch[kind + "own"] = vm((count, n_yx, rows, width), F32)
        scratch[kind + "z_r"] = vm((count, n_dp, rows, width), BF)
    names = [str(i) for i in range(13)] + list(scratch)
    vspec = pl.BlockSpec(memory_space=pltpu.VMEM)
    hspec = pl.BlockSpec(memory_space=pltpu.HBM)
    lo, gi, gp, go, gt = pl.pallas_call(
        functools.partial(kernel, n_dp, n_seq, names),
        out_shape=(
            jax.ShapeDtypeStruct((N, D), BF),
            jax.ShapeDtypeStruct((N, D), BF),
            jax.ShapeDtypeStruct((rows, 4 * D), F32),
            jax.ShapeDtypeStruct((rows, D), F32),
            jax.ShapeDtypeStruct((H, HD // 2), F32),
        ),
        in_specs=[hspec, vspec, vspec, hspec, hspec, vspec, vspec, hspec],
        out_specs=(vspec,) * 5,
        scratch_shapes=list(scratch.values()),
        compiler_params=pltpu.CompilerParams(
            collective_id=0, has_side_effects=True, vmem_limit_bytes=56 * 1024 * 1024
        ),
        name="layer",
    )(embeddings[0], user_ids, time_gaps, proj, out_w, freqs[None], mix, cot[0])
    return lo[None], gi[None], gp, go, gt


def solution(mesh):
    n_dp, n_seq = mesh.shape["dp"], mesh.shape["seq"]
    return jax.shard_map(
        functools.partial(body, n_dp, n_seq),
        mesh=mesh,
        in_specs=(
            P("dp", "seq", None),
            P("dp", "seq"),
            P("dp", "seq"),
            P(),
            P(),
            P(),
            P(),
            P("dp", "seq", None),
        ),
        out_specs=(P("dp", "seq", None), P("dp", "seq", None), P("seq", None), P("seq", None), P()),
        check_vma=False,
    )
```

time: 69.7 us -> 58.6 us (0.84); the launches traced: 69.5 us -> 57.5 us
  Pallas kernels: 60.5 us -> 51.2 us
  other arithmetic: 2.72 us -> 0 us
    pallas_call x1, Pallas kernels: 60.5 us -> 51.2 us  [body(): pl.pallas_call(functools.partial(kernel, n_dp, n_seq, names), out_shape=(...]
    concatenate x1 -> x0, other arithmetic: 1.41 us -> none  [body(): mix2 = jnp.concatenate([mix, mix], 1)]
    broadcast_in_dim x1 -> x0, other arithmetic: 1.32 us -> none  [body(): freq2 = jnp.concatenate([freqs, freqs])[None]]
where the time goes in v2:
time: 58.6 us; the launch traced here: 57.5 us
  Pallas kernels  51.2 us (87%)
  local copies, waits for them, and re-layouts  5.64 us (10%)
  between operations  0.67 us (1%)
    pallas_call x1, Pallas kernels, body(): pl.pallas_call(functools.partial(kernel, n_dp, n_seq, names), out_shape=(...  51.2 us
    unnamed x11, local copies, waits for them, and re-layouts  5.64 us

profile of v2, /device:TPU:6, one launch (start us, length us, event | category | flops | bytes accessed | tf_op | source)
XLA Modules:
  0.0 57.5 jit_solution(3954913140615939878)
XLA Ops:
  0.6 51.2 %layer.1 = (bf16[512,512]{1,0:T(8,128)(2,1)}, bf16[512,512]{1,0:T(8,128)(2,1)}, f32[16,2048]{1,0:T(8,128)}, f32[16,512]{1,0:T(8,128)}, f32[4,64]{1,0:T(4,128)}) custom-call(bf16[512,512]{1,0:T(8,128)(2,1)} %bitcast.7, s32[1,512]{1,0:T(1,128)} %refs_1_.1, s32[1,512]{1,0:T(1,128)} %refs_2_.1, bf16[512,2048]{1,0:T(8,128)(2,1)} %refs_3_.1, ...), custom_call_target="tpu_custom_call" | custom-call | tf_op jit(solution)/shard_map/layer/pallas_call | solution.py:525
  51.8 0.0 copy-start
  51.9 0.0 copy-start.1
  51.9 0.0 copy-start.2
  51.9 1.9 %copy.18 = bf16[1,512,512]{2,1,0:T(8,128)(2,1)} copy(bf16[1,512,512]{2,1,0:T(8,128)(2,1)} %bitcast.6) | data formatting | bytes 1048576
  53.8 1.9 %copy.19 = bf16[1,512,512]{2,1,0:T(8,128)(2,1)} copy(bf16[1,512,512]{2,1,0:T(8,128)(2,1)} %bitcast.5) | data formatting | bytes 1048576
  55.7 0.0 copy-done
  55.7 0.7 %copy.20 = f32[16,2048]{1,0:T(8,128)} copy(f32[16,2048]{1,0:T(8,128)S(1)} %copy-done) | data formatting | bytes 262144
  56.3 0.0 copy-done.1
  56.3 0.6 %copy.21 = f32[16,512]{1,0:T(8,128)} copy(f32[16,512]{1,0:T(8,128)S(1)} %copy-done.1) | data formatting | bytes 65536
  56.9 0.0 copy-done.2
  56.9 0.6 %copy.22 = f32[4,64]{1,0:T(4,128)} copy(f32[4,64]{1,0:T(4,128)S(1)} %copy-done.2) | data formatting | bytes 2048
Async XLA Ops:
  51.8 3.8 %copy-start = (f32[16,2048]{1,0:T(8,128)S(1)}, f32[16,2048]{1,0:T(8,128)}, u32[]{:S(2)}) copy-start(f32[16,2048]{1,0:T(8,128)} %get-tuple-element.22) | copy-start | bytes 393220
  51.9 4.5 %copy-start.1 = (f32[16,512]{1,0:T(8,128)S(1)}, f32[16,512]{1,0:T(8,128)}, u32[]{:S(2)}) copy-start(f32[16,512]{1,0:T(8,128)} %get-tuple-element.23) | copy-start | bytes 98308
  51.9 5.1 %copy-start.2 = (f32[4,64]{1,0:T(4,128)S(1)}, f32[4,64]{1,0:T(4,128)}, u32[]{:S(2)}) copy-start(f32[4,64]{1,0:T(4,128)} %get-tuple-element.24) | copy-start | bytes 3076

commit v3 on v2

--- a/solution.py
+++ b/solution.py
@@ -63,7 +63,7 @@
     gate, kcat, qcat, v4 = r["gate"], r["kcat"], r["qcat"], r["v4"]
     maskf, cs_own, wsav, slp, att4 = r["maskf"], r["cs_own"], r["wsav"], r["slp"], r["att4"]
     ggs, ga4, gpv, gpk, gpq, gpg = r["ggs"], r["ga4"], r["gpv"], r["gpk"], r["gpq"], r["gpg"]
-    back_s, back_r = r["back_s"], r["back_r"]
+    back_s, back_r, gated_s = r["back_s"], r["back_r"], r["gated_s"]
     t0_s, t0_r, t1_r, t2_r = r["t0_s"], r["t0_r"], r["t1_r"], r["t2_r"]
     in_sem, halo_ss, halo_rs = r["in_sem"], r["halo_ss"], r["halo_rs"]
     back_ss, back_rs, tm_ss, tm_rs = r["back_ss"], r["back_rs"], r["tm_ss"], r["tm_rs"]
@@ -251,6 +251,7 @@
     normed_mid = attended * scale_mid
     gate_wide = gate[...].astype(F32)
     gated = (normed_mid * gate_wide).astype(BF)
+    gated_s[...] = gated
     t4 = jnp.transpose(gated).reshape(n_yx, 2, rows, N)
     for c in range(2):
         gatt[c] = t4[:, c].reshape(half, N)
@@ -263,137 +264,170 @@
     for h in range(H):
         ga4[h] = ga[:, h * HD : (h + 1) * HD]
 
+    w_h = 2 * HD
+    tiles = (rows // 8) * (D // HD)
+    per = tiles // n_dp
+
     def part(name, c):
         return r[c[0] + name].at[c[1]]
 
-    def part_sem(name, c):
-        i = c[1] + (0 if c[0] == "o" else 2)
-        return lambda stage: r[name].at[stage, i]
-
     def stage_copy(stage, c, src, dst, dev):
-        return remote(src, dst, part_sem("st_ss", c)(stage), part_sem("st_rs", c)(stage), dev)
+        i = c[1] + (0 if c[0] == "o" else 3)
+        return remote(src, dst, r["st_ss"].at[stage, i], r["st_rs"].at[stage, i], dev)
+
+    def whole(stage, c, ref):
+        return stage_copy(stage, c, ref, ref, (dp, partner))
+
+    waits = []
+
+    def spread(stage, c, n, me, send):
+        @pl.loop(1, n)
+        def _(k):
+            peer = lax.rem(me + k, n)
+            src, dst, dev = send(peer)
+            stage_copy(stage, c, src, dst, dev).start()
+
+    def received(stage, c, ref, n):
+        copy = whole(stage, c, ref.at[pl.ds(0, n - 1)])
+        copy.wait_recv()
+        waits.append(copy)
+
+    def total_of(ref, n):
+        total = ref[0].astype(F32)
+        for i in range(1, n):
+            total = total + ref[i].astype(F32)
+        return total
 
     def s0_copy(c):
         return stage_copy(0, c, part("s0_s", c), part("s0_r", c), (dp, partner))
 
     def stage0(c, grad):
-        width = 512 if c[0] == "o" else 3 * HD
-        part("s0_s", c)[...] = grad(1 - core).reshape(n_yx, rows, width).astype(BF)
+        shape = (n_yx, rows, D if c[0] == "o" else w_h)
+        part("s0_s", c)[...] = grad(1 - core).reshape(shape).astype(BF)
         s0_copy(c).start()
-        part("own", c)[...] = grad(core).reshape(n_yx, rows, width)
-
-    def stage1(c):
-        s0_copy(c).wait_recv()
-        s1_s, s1_r = part("s1_s", c), part("s1_r", c)
-        s1_s[...] = (part("own", c)[...] + part("s0_r", c)[...].astype(F32)).astype(BF)
-        s1_r[m] = s1_s[m]
-
-        @pl.loop(1, n_yx)
-        def _(k):
-            peer = lax.rem(m + k, n_yx)
-            stage_copy(1, c, s1_s.at[peer], s1_r.at[m], yx_dev(peer)).start()
-
-    yx_part = pl.ds(0, n_yx - 1)
-    z_part = pl.ds(0, n_dp - 1)
-
-    def s1_all(c):
-        ref = part("s1_r", c).at[yx_part]
-        return stage_copy(1, c, ref, ref, (dp, partner))
-
-    def z_all(c):
-        ref = part("z_r", c).at[z_part]
-        return stage_copy(2, c, ref, ref, (dp, partner))
-
-    def stage2(c):
-        s1_all(c).wait_recv()
-        s1_r, z_r = part("s1_r", c), part("z_r", c)
-        total = s1_r[0].astype(F32)
-        for i in range(1, n_yx):
-            total = total + s1_r[i].astype(F32)
-        z_r[dp] = total.astype(BF)
-
-        @pl.loop(1, n_dp)
-        def _(k):
-            peer = lax.rem(dp + k, n_dp)
-            stage_copy(2, c, z_r.at[dp], z_r.at[dp], z_dev(peer)).start()
+        part("own", c)[...] = grad(core).reshape(shape)
+
+    def pair_sum(c):
+        copy = s0_copy(c)
+        copy.wait_recv()
+        waits.append(copy)
+        return (part("own", c)[...] + part("s0_r", c)[...].astype(F32)).astype(BF)
+
+    def h1(c):
+        s_ref, r_ref = part("s1_s", c), part("s1_r", c)
+        s_ref[...] = pair_sum(c)
+        r_ref[m] = s_ref[m]
+        spread(1, c, n_yx, m, lambda p: (s_ref.at[p], r_ref.at[m], yx_dev(p)))
+
+    def o3(c):
+        s_ref, r_ref = part("z_s", c), part("z_r", c)
+        received(1, c, part("s1_r", c), n_yx)
+        total = total_of(part("s1_r", c), n_yx).astype(BF)
+        for i in range(tiles):
+            at, col = i // (D // HD) * 8, i % (D // HD) * HD
+            s_ref[i // per, i % per] = total[at : at + 8, col : col + HD]
+        r_ref[dp] = s_ref[dp]
+        spread(3, c, n_dp, dp, lambda p: (s_ref.at[p], r_ref.at[dp], z_dev(p)))
+
+    def o4(c):
+        r_ref = part("g_r", c)
+        received(3, c, part("z_r", c), n_dp)
+        r_ref[dp] = total_of(part("z_r", c), n_dp).astype(BF)
+        spread(4, c, n_dp, dp, lambda p: (r_ref.at[dp], r_ref.at[dp], z_dev(p)))
 
     factor = float(n_dp * n_seq * N) ** -0.5
 
-    def stage3(c):
-        z_all(c).wait_recv()
-        z_r = part("z_r", c)
-        total = z_r[0].astype(F32)
-        for i in range(1, n_dp):
-            total = total + z_r[i].astype(F32)
-        total = total * factor
-        if c == ("o", 0):
-            go_out[...] = total
-        elif c == ("o", 1):
-            gp_out[:, :D] = total
-        else:
-            for i in range(3):
-                at = (1 + i) * D + c[1] * HD
-                gp_out[:, at : at + HD] = total[:, i * HD : (i + 1) * HD]
-
-    out_c, gate_c = ("o", 0), ("o", 1)
+    def o5(c):
+        r_ref = part("g_r", c)
+        received(4, c, r_ref, n_dp)
+        for i in range(tiles):
+            at, col = i // (D // HD) * 8, i % (D // HD) * HD
+            tile = r_ref[i // per, i % per].astype(F32) * factor
+            if c[1] == 0:
+                go_out[at : at + 8, col : col + HD] = tile
+            else:
+                base = (c[1] - 1) * D + col
+                gp_out[at : at + 8, base : base + HD] = tile
+
+    def h2(c):
+        r_ref = part("z_r", c)
+        received(1, c, part("s1_r", c), n_yx)
+        r_ref[dp] = total_of(part("s1_r", c), n_yx).astype(BF)
+        spread(2, c, n_dp, dp, lambda p: (r_ref.at[dp], r_ref.at[dp], z_dev(p)))
+
+    def h3(c):
+        received(2, c, part("z_r", c), n_dp)
+        total = total_of(part("z_r", c), n_dp) * factor
+        gp_out[:, 2 * D + c[1] * HD : 2 * D + (c[1] + 1) * HD] = total[:, :HD]
+        gp_out[:, 3 * D + c[1] * HD : 3 * D + (c[1] + 1) * HD] = total[:, HD:]
+
+    out_c, gate_c, val_c = ("o", 0), ("o", 1), ("o", 2)
+    hc = [("h", h) for h in range(H)]
     stage0(out_c, lambda c: nn(gatt[c], cotv[...]))
     stage0(gate_c, lambda c: nn(nrmt[c, :, N:], gpg[...]))
     put_nrmt(0, N)
-    lo_ref[...] = (xv[...].astype(F32) + nn(gated, wov[...])).astype(BF)
+
+    def put_window(dst, t, sl, f, cols):
+        dst[:TQ, cols] = (t[0][:TQ] * (sl[:TQ, cols] * f)).astype(BF)
+        dst[TQ:WIN, cols] = ((t[0][TQ:] + t[1][:N]) * (sl[TQ:WIN, cols] * f)).astype(BF)
+        dst[WIN:, cols] = (t[1][N:] * (sl[WIN:, cols] * f)).astype(BF)
+
+    for h in range(H):
+        t = [
+            tn(wsav[h, q0 : q0 + TQ, :], ga4[h, q0 : q0 + TQ, :]) for q0 in range(0, N, TQ)
+        ]
+        put_window(gpv, t, sl_v, 1.0, slice(h * HD, (h + 1) * HD))
+    h1(out_c)
+    stage0(val_c, lambda c: nn(nrmt[c], gpv[...]))
 
     rowid = lax.broadcasted_iota(jnp.int32, (8, HD), 0)
 
-    def head(h, tm):
+    def head(h, tm, *between):
         cols = slice(h * HD, (h + 1) * HD)
-        tv, tk = [], []
+        tk = []
         for a in range(N // TQ):
             q0, k0 = a * TQ, a * TQ
-            gah = ga4[h, q0 : q0 + TQ, :]
-            gw = nt(gah, v4[h, k0 : k0 + WIN, :])
+            gw = nt(ga4[h, q0 : q0 + TQ, :], v4[h, k0 : k0 + WIN, :])
             gs = (gw * slp[h, q0 : q0 + TQ, :]).astype(BF)
-            tv.append(tn(wsav[h, q0 : q0 + TQ, :], gah))
             tk.append(tn(gs, qcat[h, q0 : q0 + TQ, :HD]))
             dqc = nn(gs, kcat[h, k0 : k0 + WIN, :])
             gpq[q0 : q0 + TQ, cols] = (dqc[:, :HD] * (sl_q[q0 : q0 + TQ, cols] * inv)).astype(BF)
             got = jnp.sum(dqc[:, HD:] * cs_own[q0 : q0 + TQ, :], 0, keepdims=True)
             tm = tm + jnp.where(rowid == h, got, 0.0)
-        for dst, t, sl, f in ((gpv, tv, sl_v, 1.0), (gpk, tk, sl_k, inv)):
-            dst[:TQ, cols] = (t[0][:TQ] * (sl[:TQ, cols] * f)).astype(BF)
-            dst[TQ:WIN, cols] = ((t[0][TQ:] + t[1][:N]) * (sl[TQ:WIN, cols] * f)).astype(BF)
-            dst[WIN:, cols] = (t[1][N:] * (sl[WIN:, cols] * f)).astype(BF)
+            if a == 0:
+                for step, c in between:
+                    step(c)
+        put_window(gpk, tk, sl_k, inv, cols)
         return tm
 
     def head_grad(h):
         cols = slice(h * HD, (h + 1) * HD)
 
         def grad(c):
-            vk = nn(nrmt[c], jnp.concatenate([gpv[:, cols], gpk[:, cols]], 1))
-            q = nn(nrmt[c, :, N:], gpq[:, cols])
-            return jnp.concatenate([vk[:, :HD], q, vk[:, HD:]], 1)
+            own = nn(nrmt[c, :, N:], jnp.concatenate([gpq[:, cols], gpk[N:, cols]], 1))
+            prev = nn(nrmt[c, :, :N], gpk[:N, cols])
+            return jnp.concatenate([own[:, :HD], own[:, HD:] + prev], 1)
 
         return grad
 
-    hc = [("h", h) for h in range(H)]
-    tm = head(0, jnp.zeros((8, HD), F32))
-    stage1(out_c)
+    tm = head(0, jnp.zeros((8, HD), F32), (h1, gate_c))
+    h1(val_c)
     stage0(hc[0], head_grad(0))
     tm = head(1, tm)
-    stage1(gate_c)
-    stage1(hc[0])
+    h1(hc[0])
     stage0(hc[1], head_grad(1))
     tm = head(2, tm)
-    stage1(hc[1])
-    stage2(out_c)
+    h1(hc[1])
     stage0(hc[2], head_grad(2))
-    tm = head(3, tm)
-    stage1(hc[2])
-    stage2(gate_c)
+    tm = head(3, tm, (o3, out_c))
+    h1(hc[2])
     t0_s[...] = tm
     tm0 = remote(t0_s, t0_r, tm_ss.at[0], tm_rs.at[0], (dp, partner))
     tm0.start()
     stage0(hc[3], head_grad(3))
+    o3(gate_c)
     back_s[...] = (nt(gpv[:N, :], wv[:, D : 2 * D]) + nt(gpk[:N, :], wv[:, 3 * D :])).astype(BF)
-    stage2(hc[0])
+    h1(hc[3])
     tm0.wait_recv()
     t1_r[m] = t0_s[...] + t0_r[...]
 
@@ -402,22 +436,26 @@
         peer = lax.rem(m + k, n_yx)
         remote(t1_r.at[m], t1_r.at[m], tm_ss.at[1], tm_rs.at[1], yx_dev(peer)).start()
 
-    stage1(hc[3])
     back = remote(back_s, back_r, back_ss.at[0], back_rs.at[0], (dp, left))
     back.start()
-    stage2(hc[1])
-    gn = (
+    o3(val_c)
+    h2(hc[0])
+    lo_ref[...] = (xv[...].astype(F32) + nn(gated_s[...], wov[...])).astype(BF)
+    ggs[...] = (
         nt(gpg[...], wv[:, :D])
         + nt(gpv[N:, :], wv[:, D : 2 * D])
         + nt(gpq[...], wv[:, 2 * D : 3 * D])
         + nt(gpk[N:, :], wv[:, 3 * D :])
     )
-    ggs[...] = gn
+    h2(hc[1])
+    o4(out_c)
+    h2(hc[2])
+    o4(gate_c)
 
     def tm_all(ref, i):
         return remote(ref, ref, tm_ss.at[i], tm_rs.at[i], (dp, partner))
 
-    tm1, tm2 = tm_all(t1_r.at[yx_part], 1), tm_all(t2_r.at[z_part], 2)
+    tm1, tm2 = tm_all(t1_r.at[pl.ds(0, n_yx - 1)], 1), tm_all(t2_r.at[pl.ds(0, n_dp - 1)], 2)
     tm1.wait_recv()
     tsum = t1_r[0]
     for i in range(1, n_yx):
@@ -429,11 +467,8 @@
         peer = lax.rem(dp + k, n_dp)
         remote(t2_r.at[dp], t2_r.at[dp], tm_ss.at[2], tm_rs.at[2], z_dev(peer)).start()
 
-    stage2(hc[2])
-    stage3(out_c)
-    stage3(gate_c)
-    stage2(hc[3])
-    stage3(hc[0])
+    o4(val_c)
+    h2(hc[3])
     back.wait_recv()
     wide, scale = norm(xv[...])
     unit = wide * scale
@@ -441,26 +476,31 @@
     gi_ref[...] = (
         cotv[...].astype(F32) + scale * (gn - unit * jnp.mean(gn * unit, -1, keepdims=True))
     ).astype(BF)
-    stage3(hc[1])
-    stage3(hc[2])
+    h3(hc[0])
+    h3(hc[1])
+    h3(hc[2])
+    o5(out_c)
+    o5(gate_c)
+    o5(val_c)
     tm2.wait_recv()
     tsum = t2_r[0]
     for i in range(1, n_dp):
         tsum = tsum + t2_r[i]
     tsum = (tsum + pltpu.roll(tsum, HD // 2, 1)) * factor
     gt_out[...] = tsum[:H, : HD // 2]
-    stage3(hc[3])
-
-    for copy in halo:
+    h3(hc[3])
+
+    for copy in halo + [back, tm0, tm1, tm2] + waits:
         copy.wait_send()
-    back.wait_send()
-    tm0.wait_send()
-    tm1.wait_send()
-    tm2.wait_send()
-    for c in [out_c, gate_c] + hc:
-        s0_copy(c).wait_send()
-        s1_all(c).wait_send()
-        z_all(c).wait_send()
+
+
+def store(*refs):
+    sems = refs[10]
+    copies = [pltpu.make_async_copy(refs[i], refs[5 + i], sems.at[i]) for i in range(5)]
+    for copy in copies:
+        copy.start()
+    for copy in copies:
+        copy.wait()
 
 
 def body(n_dp, n_seq, embeddings, user_ids, time_gaps, proj, out_w, freqs, mix, cot):
@@ -498,6 +538,7 @@
         "gpk": vm((2 * N, D), BF),
         "gpq": vm((N, D), BF),
         "gpg": vm((N, D), BF),
+        "gated_s": vm((N, D), BF),
         "back_s": vm((N, D), BF),
         "back_r": vm((N, D), BF),
         "t0_s": vm((8, HD), F32),
@@ -509,28 +550,32 @@
         "halo_rs": dma((4,)),
         "back_ss": dma((1,)),
         "back_rs": dma((1,)),
-        "st_ss": dma((3, 2 + H)),
-        "st_rs": dma((3, 2 + H)),
+        "st_ss": dma((5, 3 + H)),
+        "st_rs": dma((5, 3 + H)),
         "tm_ss": dma((3,)),
         "tm_rs": dma((3,)),
     }
-    for kind, count, width in (("o", 2, D), ("h", H, 3 * HD)):
+    per = (rows // 8) * (D // HD) // n_dp
+    for kind, count, width in (("o", 3, D), ("h", H, 2 * HD)):
         for name in ("s0_s", "s0_r", "s1_s", "s1_r"):
             scratch[kind + name] = vm((count, n_yx, rows, width), BF)
         scratch[kind + "own"] = vm((count, n_yx, rows, width), F32)
-        scratch[kind + "z_r"] = vm((count, n_dp, rows, width), BF)
+    for name in ("z_s", "z_r", "g_r"):
+        scratch["o" + name] = vm((3, n_dp, per, 8, HD), BF)
+    scratch["hz_r"] = vm((H, n_dp, rows, 2 * HD), BF)
     names = [str(i) for i in range(13)] + list(scratch)
     vspec = pl.BlockSpec(memory_space=pltpu.VMEM)
     hspec = pl.BlockSpec(memory_space=pltpu.HBM)
-    lo, gi, gp, go, gt = pl.pallas_call(
+    results = (
+        ((N, D), BF),
+        ((N, D), BF),
+        ((rows, 4 * D), F32),
+        ((rows, D), F32),
+        ((H, HD // 2), F32),
+    )
+    held = pl.pallas_call(
         functools.partial(kernel, n_dp, n_seq, names),
-        out_shape=(
-            jax.ShapeDtypeStruct((N, D), BF),
-            jax.ShapeDtypeStruct((N, D), BF),
-            jax.ShapeDtypeStruct((rows, 4 * D), F32),
-            jax.ShapeDtypeStruct((rows, D), F32),
-            jax.ShapeDtypeStruct((H, HD // 2), F32),
-        ),
+        out_shape=tuple(vm(shape, dtype) for shape, dtype in results),
         in_specs=[hspec, vspec, vspec, hspec, hspec, vspec, vspec, hspec],
         out_specs=(vspec,) * 5,
         scratch_shapes=list(scratch.values()),
@@ -539,6 +584,15 @@
         ),
         name="layer",
     )(embeddings[0], user_ids, time_gaps, proj, out_w, freqs[None], mix, cot[0])
+    lo, gi, gp, go, gt = pl.pallas_call(
+        store,
+        out_shape=tuple(jax.ShapeDtypeStruct(shape, dtype) for shape, dtype in results),
+        in_specs=[vspec] * 5,
+        out_specs=(hspec,) * 5,
+        scratch_shapes=[dma((5,))],
+        compiler_params=pltpu.CompilerParams(vmem_limit_bytes=4 * 1024 * 1024),
+        name="store",
+    )(*held)
     return lo[None], gi[None], gp, go, gt
 
 

time: 58.6 us -> 51 us (0.87); the launches traced: 57.5 us -> 50.6 us
  local copies, waits for them, and re-layouts: 5.64 us -> 0 us
  Pallas kernels: 51.2 us -> 49.8 us
    unnamed x11 -> x0, local copies, waits for them, and re-layouts: 5.64 us -> none
    pallas_call x1 -> x2, Pallas kernels: 51.2 us -> 49.8 us  [the longest x1 48.8 us: body(): pl.pallas_call(functools.partial(kernel, n_dp, n_seq, names), out_shape=t...]
where the time goes in v3:
time: 51 us; the launch traced here: 50.6 us
  Pallas kernels  49.8 us (98%)
  between operations  0.8 us (2%)
    pallas_call x1, Pallas kernels, body(): pl.pallas_call(functools.partial(kernel, n_dp, n_seq, names), out_shape=t...  48.8 us
    pallas_call x1, Pallas kernels, body(): pl.pallas_call(store, out_shape=tuple((jax.ShapeDtypeStruct(shape, dtype)...  1.05 us

profile of v3, /device:TPU:6, one launch (start us, length us, event | category | flops | bytes accessed | tf_op | source)
XLA Modules:
  0.0 50.6 jit_solution(6103441167954078718)
XLA Ops:
  0.6 48.8 %layer.1 = (bf16[512,512]{1,0:T(8,128)(2,1)S(1)}, bf16[512,512]{1,0:T(8,128)(2,1)S(1)}, f32[16,2048]{1,0:T(8,128)S(1)}, f32[16,512]{1,0:T(8,128)S(1)}, f32[4,64]{1,0:T(4,128)S(1)}) custom-call(bf16[512,512]{1,0:T(8,128)(2,1)} %bitcast.5, s32[1,512]{1,0:T(1,128)} %refs_1_.1, s32[1,512]{1,0:T(1,128)} %refs_2_.1, bf16[512,2048]{1,0:T(8,128)(2,1)} %refs_3_.1, ...), custom_call_target="tpu_custom_call" | custom-call | tf_op jit(solution)/shard_map/layer/pallas_call | solution.py:576
  49.4 1.1 %store.1 = (bf16[512,512]{1,0:T(8,128)(2,1)}, bf16[512,512]{1,0:T(8,128)(2,1)}, f32[16,2048]{1,0:T(8,128)}, f32[16,512]{1,0:T(8,128)}, f32[4,64]{1,0:T(4,128)}) custom-call(bf16[512,512]{1,0:T(8,128)(2,1)S(1)} %get-tuple-element.15.refs_0_, bf16[512,512]{1,0:T(8,128)(2,1)S(1)} %get-tuple-element.16.refs_1_, f32[16,2048]{1,0:T(8,128)S(1)} %get-tuple-element.17.refs_2_, ...), custom_call_target="tpu_custom_call" | custom-call | tf_op jit(solution)/shard_map/store/pallas_call | solution.py:587

commit v4 on v3

--- a/solution.py
+++ b/solution.py
@@ -104,6 +104,10 @@
         pltpu.make_async_copy(w_ref, wv, in_sem.at[1]),
         pltpu.make_async_copy(wo_ref, wov, in_sem.at[2]),
         pltpu.make_async_copy(cot_ref, cotv, in_sem.at[3]),
+        pltpu.make_async_copy(u_ref, r["uv"], in_sem.at[4]),
+        pltpu.make_async_copy(g_ref, r["gv"], in_sem.at[5]),
+        pltpu.make_async_copy(f_ref, r["fv"], in_sem.at[6]),
+        pltpu.make_async_copy(mix_ref, r["mv"], in_sem.at[7]),
     ]
     for copy in loads:
         copy.start()
@@ -115,8 +119,8 @@
 
     hi, lo = pl.ds(TQ, TQ), pl.ds(0, TQ)
     halo = [
-        remote(u_ref, uprev, halo_ss.at[0], halo_rs.at[0], (dp, right)),
-        remote(g_ref, gprev, halo_ss.at[1], halo_rs.at[1], (dp, right)),
+        remote(r["uv"], uprev, halo_ss.at[0], halo_rs.at[0], (dp, right)),
+        remote(r["gv"], gprev, halo_ss.at[1], halo_rs.at[1], (dp, right)),
         remote(xv.at[hi], xp.at[hi], halo_ss.at[2], halo_rs.at[2], (dp, right)),
         remote(xv.at[lo], xp.at[lo], halo_ss.at[3], halo_rs.at[3], (dp, right)),
     ]
@@ -158,6 +162,8 @@
     gate[...] = hid
     sl_g[...] = sl
 
+    for copy in loads[4:]:
+        copy.wait()
     pl.semaphore_wait(barrier, 3 + (n_yx - 1) + (n_dp - 1))
     for copy in halo:
         copy.start()
@@ -173,15 +179,15 @@
 
     halo[0].wait_recv()
     halo[1].wait_recv()
-    u_own = u_ref[...].astype(F32)
+    u_own = r["uv"][...].astype(F32)
     u_prev = jnp.where(s == 0, -1.0, uprev[...].astype(F32))
-    g_own = g_ref[...].astype(F32)
+    g_own = r["gv"][...].astype(F32)
     g_prev = gprev[...].astype(F32)
     u_all = jnp.concatenate([u_prev, u_own], 1)
     g_all = jnp.broadcast_to(jnp.concatenate([g_prev, g_own], 1), (HD, 2 * N)).astype(BF)
     uc = jnp.transpose(jnp.broadcast_to(u_all, (HD, 2 * N)))[:, :1]
-    freq = jnp.concatenate([f_ref[...], f_ref[...]], 1)
-    mix = jnp.concatenate([mix_ref[...], mix_ref[...]], 1) * (HD**0.5)
+    freq = jnp.concatenate([r["fv"][...], r["fv"][...]], 1)
+    mix = jnp.concatenate([r["mv"][...], r["mv"][...]], 1) * (HD**0.5)
     lane = lax.broadcasted_iota(jnp.int32, (1, HD), 1)
     shift = jnp.where(lane < HD // 2, 0.0, 0.5)
 
@@ -194,7 +200,7 @@
         qpos = lax.broadcasted_iota(jnp.int32, (TQ, WIN), 0) + (q0 + N)
         same = uc[N + q0 : N + q0 + TQ, :] == u_all[:, k0 : k0 + WIN]
         mk = jnp.where(same & (kpos <= qpos), 1.0, 0.0)
-        maskf[q0 : q0 + TQ, :] = mk
+        maskf[q0 : q0 + TQ, :] = 0.5 * mk
         feat = features(nt(mk.astype(BF), g_all[:, k0 : k0 + WIN]))
         cs_own[q0 : q0 + TQ, :] = feat
         fb = feat.astype(BF)
@@ -214,7 +220,7 @@
         q0 = a * TQ
         k0 = q0 + col
         z = nt(qcat[h, q0 : q0 + TQ, :], kcat[h, k0 : k0 + n, :]) * inv
-        sg = sigmoid(z) * maskf[q0 : q0 + TQ, col : col + n]
+        sg = (jnp.tanh(0.5 * z) + 1.0) * maskf[q0 : q0 + TQ, col : col + n]
         wt = z * sg
         slp[h, q0 : q0 + TQ, col : col + n] = sg + wt * (1.0 - sg)
         wb = wt.astype(BF)
@@ -545,7 +551,11 @@
         "t0_r": vm((8, HD), F32),
         "t1_r": vm((n_yx, 8, HD), F32),
         "t2_r": vm((n_dp, 8, HD), F32),
-        "in_sem": dma((4,)),
+        "uv": vm((1, N), jnp.int32),
+        "gv": vm((1, N), jnp.int32),
+        "fv": vm((1, HD // 2), F32),
+        "mv": vm((H, HD // 2), F32),
+        "in_sem": dma((8,)),
         "halo_ss": dma((4,)),
         "halo_rs": dma((4,)),
         "back_ss": dma((1,)),
@@ -576,7 +586,7 @@
     held = pl.pallas_call(
         functools.partial(kernel, n_dp, n_seq, names),
         out_shape=tuple(vm(shape, dtype) for shape, dtype in results),
-        in_specs=[hspec, vspec, vspec, hspec, hspec, vspec, vspec, hspec],
+        in_specs=[hspec] * 8,
         out_specs=(vspec,) * 5,
         scratch_shapes=list(scratch.values()),
         compiler_params=pltpu.CompilerParams(

time: 51 us -> 50.2 us (0.984)
  Pallas kernels: 49.8 us -> 49.1 us
    pallas_call x1, Pallas kernels: 48.8 us -> 48.1 us  [body(): pl.pallas_call(functools.partial(kernel, n_dp, n_seq, names), out_shape=t...]
where the time goes in v4:
time: 50.2 us; the launch traced here: 49.9 us
  Pallas kernels  49.1 us (98%)
  between operations  0.8 us (2%)
    pallas_call x1, Pallas kernels, body(): pl.pallas_call(functools.partial(kernel, n_dp, n_seq, names), out_shape=t...  48.1 us
    pallas_call x1, Pallas kernels, body(): pl.pallas_call(store, out_shape=tuple((jax.ShapeDtypeStruct(shape, dtype)...  1.05 us

profile of v4, /device:TPU:6, one launch (start us, length us, event | category | flops | bytes accessed | tf_op | source)
XLA Modules:
  0.0 49.9 jit_solution(915228062435850500)
XLA Ops:
  0.6 48.1 %layer.1 = (bf16[512,512]{1,0:T(8,128)(2,1)S(1)}, bf16[512,512]{1,0:T(8,128)(2,1)S(1)}, f32[16,2048]{1,0:T(8,128)S(1)}, f32[16,512]{1,0:T(8,128)S(1)}, f32[4,64]{1,0:T(4,128)S(1)}) custom-call(bf16[512,512]{1,0:T(8,128)(2,1)} %bitcast.5, s32[1,512]{1,0:T(1,128)} %refs_1_.1, s32[1,512]{1,0:T(1,128)} %refs_2_.1, bf16[512,2048]{1,0:T(8,128)(2,1)} %refs_3_.1, ...), custom_call_target="tpu_custom_call" | custom-call | tf_op jit(solution)/shard_map/layer/pallas_call | solution.py:586
  48.7 1.1 %store.1 = (bf16[512,512]{1,0:T(8,128)(2,1)}, bf16[512,512]{1,0:T(8,128)(2,1)}, f32[16,2048]{1,0:T(8,128)}, f32[16,512]{1,0:T(8,128)}, f32[4,64]{1,0:T(4,128)}) custom-call(bf16[512,512]{1,0:T(8,128)(2,1)S(1)} %get-tuple-element.15.refs_0_, bf16[512,512]{1,0:T(8,128)(2,1)S(1)} %get-tuple-element.16.refs_1_, f32[16,2048]{1,0:T(8,128)S(1)} %get-tuple-element.17.refs_2_, ...), custom_call_target="tpu_custom_call" | custom-call | tf_op jit(solution)/shard_map/store/pallas_call | solution.py:597

commit v5 on v4

--- a/solution.py
+++ b/solution.py
@@ -287,9 +287,9 @@
     waits = []
 
     def spread(stage, c, n, me, send):
-        @pl.loop(1, n)
+        @pl.loop(0, n - 1)
         def _(k):
-            peer = lax.rem(me + k, n)
+            peer = lax.rem(me + 1 + lax.rem(k + n // 2 - 1, n - 1), n)
             src, dst, dev = send(peer)
             stage_copy(stage, c, src, dst, dev).start()
 

time: 50.2 us -> 50.5 us (level)
  no operation moved by 1% of the time
where the time goes in v5:
time: 50.5 us; the launch traced here: 49.9 us
  Pallas kernels  49 us (97%)
  between operations  0.8 us (2%)
    pallas_call x1, Pallas kernels, body(): pl.pallas_call(functools.partial(kernel, n_dp, n_seq, names), out_shape=t...  48 us
    pallas_call x1, Pallas kernels, body(): pl.pallas_call(store, out_shape=tuple((jax.ShapeDtypeStruct(shape, dtype)...  1.05 us

profile of v5, /device:TPU:6, one launch (start us, length us, event | category | flops | bytes accessed | tf_op | source)
XLA Modules:
  0.0 49.9 jit_solution(12799097397110778180)
XLA Ops:
  0.6 48.0 %layer.1 = (bf16[512,512]{1,0:T(8,128)(2,1)S(1)}, bf16[512,512]{1,0:T(8,128)(2,1)S(1)}, f32[16,2048]{1,0:T(8,128)S(1)}, f32[16,512]{1,0:T(8,128)S(1)}, f32[4,64]{1,0:T(4,128)S(1)}) custom-call(bf16[512,512]{1,0:T(8,128)(2,1)} %bitcast.5, s32[1,512]{1,0:T(1,128)} %refs_1_.1, s32[1,512]{1,0:T(1,128)} %refs_2_.1, bf16[512,2048]{1,0:T(8,128)(2,1)} %refs_3_.1, ...), custom_call_target="tpu_custom_call" | custom-call | tf_op jit(solution)/shard_map/layer/pallas_call | solution.py:586
  48.6 1.1 %store.1 = (bf16[512,512]{1,0:T(8,128)(2,1)}, bf16[512,512]{1,0:T(8,128)(2,1)}, f32[16,2048]{1,0:T(8,128)}, f32[16,512]{1,0:T(8,128)}, f32[4,64]{1,0:T(4,128)}) custom-call(bf16[512,512]{1,0:T(8,128)(2,1)S(1)} %get-tuple-element.15.refs_0_, bf16[512,512]{1,0:T(8,128)(2,1)S(1)} %get-tuple-element.16.refs_1_, f32[16,2048]{1,0:T(8,128)S(1)} %get-tuple-element.17.refs_2_, ...), custom_call_target="tpu_custom_call" | custom-call | tf_op jit(solution)/shard_map/store/pallas_call | solution.py:597
